TPU v7x, 32 devices: a whole 2x2x4 slice. The times are simulated.
32 devices in a mesh: fsdp: 8 (over y, x, core), tp: 4 (over z).
Axes of the slice: x: 2, y: 2, z: 4, core: 2. Of those that a mesh axis runs over, the one named last changes fastest.
Arguments:
- tokens: bfloat16 [8192, 768], P(('fsdp', 'tp')), may hold values from -6 to 6
- segment_ids: int32 [8, 1024], P('fsdp'), may hold values from 0 to 7, never falling along the last dimension, each value on 1 to 384 neighbouring positions
- patch_pos: int32 [2, 8192], P(None, ('fsdp', 'tp')), may hold values from 0 to 63
- row_table: bfloat16 [64, 768], P(None, ('fsdp', 'tp')), may hold values from -3 to 3
- col_table: bfloat16 [64, 768], P(None, ('fsdp', 'tp')), may hold values from -3 to 3
- ln_gain: bfloat16 [2, 2, 768], P(None, None, ('fsdp', 'tp')), may hold values from 0.5 to 1.5
- ln_bias: bfloat16 [2, 2, 768], P(None, None, ('fsdp', 'tp')), may hold values from -1.796875 to 1.796875
- qkv_bias: bfloat16 [2, 3, 768], P(None, None, ('fsdp', 'tp')), may hold values from -1.796875 to 1.796875
- qk_gain: bfloat16 [2, 2, 768], P(None, None, ('fsdp', 'tp')), may hold values from 0.5 to 1.5
- query_bias: bfloat16 [2, 768], P(None, ('fsdp', 'tp')), may hold values from -3 to 3
- out_bias: bfloat16 [2, 768], P(None, ('fsdp', 'tp')), may hold values from -1.796875 to 1.796875
- fc1_bias: bfloat16 [2, 3072], P(None, ('fsdp', 'tp')), may hold values from -1.796875 to 1.796875
- fc2_bias: bfloat16 [2, 768], P(None, ('fsdp', 'tp')), may hold values from -1.796875 to 1.796875
- w_qkv: bfloat16 [2, 768, 3, 768], P(None, 'fsdp', None, 'tp'), may hold values from -0.21875 to 0.21875
- w_out: bfloat16 [2, 768, 768], P(None, 'tp', 'fsdp'), may hold values from -1.75 to 1.75
- w_fc1: bfloat16 [2, 768, 3072], P(None, 'fsdp', 'tp'), may hold values from -0.21875 to 0.21875
- w_fc2: bfloat16 [2, 3072, 768], P(None, 'tp', 'fsdp'), may hold values from -0.109375 to 0.109375
- cotangent: float32 [8192, 768], P(('fsdp', 'tp')), may hold values from -6 to 6
Outputs:
- activations: float32 [8192, 768], P(('fsdp', 'tp'))
- token_grad: float32 [8192, 768], P(('fsdp', 'tp'))
- row_table_grad: float32 [64, 768], P(None, ('fsdp', 'tp'))
- col_table_grad: float32 [64, 768], P(None, ('fsdp', 'tp'))
- ln_gain_grad: float32 [2, 2, 768], P(None, None, ('fsdp', 'tp'))
- ln_bias_grad: float32 [2, 2, 768], P(None, None, ('fsdp', 'tp'))
- qkv_bias_grad: float32 [2, 3, 768], P(None, None, ('fsdp', 'tp'))
- qk_gain_grad: float32 [2, 2, 768], P(None, None, ('fsdp', 'tp'))
- query_bias_grad: float32 [2, 768], P(None, ('fsdp', 'tp'))
- out_bias_grad: float32 [2, 768], P(None, ('fsdp', 'tp'))
- fc1_bias_grad: float32 [2, 3072], P(None, ('fsdp', 'tp'))
- fc2_bias_grad: float32 [2, 768], P(None, ('fsdp', 'tp'))
- w_qkv_grad: float32 [2, 768, 3, 768], P(None, 'fsdp', None, 'tp')
- w_out_grad: float32 [2, 768, 768], P(None, 'tp', 'fsdp')
- w_fc1_grad: float32 [2, 768, 3072], P(None, 'fsdp', 'tp')
- w_fc2_grad: float32 [2, 3072, 768], P(None, 'tp', 'fsdp')
Inputs may be any that keep to these rules, and one draw needn't show every extreme that they name: `segment_ids`: each row is one sequence; ids never fall along it and every id from 0 to 7 appears in one run of 1 to 384 tokens; some image has exactly 384.
All inputs are finite; a program needn't handle non-finite values.
Results may differ from a plain program's by a relative error of at most 0.019.
Values may be sent and summed in bfloat16 or wider, within the bound.
A program may use at most 192 MiB of HBM per device.

v0:
```python
import functools

import jax
import jax.numpy as jnp
from jax import lax
from jax.experimental import pallas as pl
from jax.experimental.pallas import tpu as pltpu
from jax.sharding import PartitionSpec as P

HD = 64
PAIR = 128
REACH = 384
EPS = 1e-06
FILL = -1e30
ROOT_HALF = 0.7071067811865476
INV_ROOT_TWO_PI = 0.3989422804014327
HIGHEST = lax.Precision.HIGHEST
F32 = jnp.float32
BF16 = jnp.bfloat16
MESH = pl.DeviceIdType.MESH
VMEM = 67043328
ANY = pl.BlockSpec(memory_space=pl.ANY)


def nn(left, right):
    return lax.dot_general(left, right, (((1,), (0,)), ((), ())), preferred_element_type=F32)


def nt(left, right):
    return lax.dot_general(left, right, (((1,), (1,)), ((), ())), preferred_element_type=F32)


def halves(array):
    middle = array.shape[1] // 2
    return array[:, :middle], array[:, middle:]


def row_norm(value):
    centered = value - jnp.mean(value, axis=-1, keepdims=True)
    scale = lax.rsqrt(jnp.mean(centered * centered, axis=-1, keepdims=True) + EPS)
    return centered * scale, scale


def row_norm_back(grad_hat, normed, scale):
    return scale * (
        grad_hat
        - jnp.mean(grad_hat, axis=-1, keepdims=True)
        - normed * jnp.mean(grad_hat * normed, axis=-1, keepdims=True)
    )


def head_mean(value, exact=False):
    wide = value.shape[1]
    rows = lax.broadcasted_iota(jnp.int32, (wide, wide), 0) // HD
    cols = lax.broadcasted_iota(jnp.int32, (wide, wide), 1) // HD
    spread = jnp.where(rows == cols, 1.0 / HD, 0.0).astype(BF16)
    high = value.astype(BF16)
    mean = nn(high, spread)
    if exact:
        mean += nn((value - high.astype(F32)).astype(BF16), spread)
    return mean


def head_norm(value):
    centered = value - head_mean(value, exact=True)
    scale = lax.rsqrt(head_mean(centered * centered) + EPS)
    return centered * scale, scale


def head_norm_back(grad_hat, normed, scale):
    return scale * (grad_hat - head_mean(grad_hat) - normed * head_mean(grad_hat * normed))


def only(array, part):
    return jnp.where(lax.broadcasted_iota(jnp.int32, (1, PAIR), 1) // HD == part, array, jnp.zeros_like(array))


def side(*parts):
    return jnp.concatenate(parts, axis=1)


def whole(shape):
    return pl.BlockSpec(shape, lambda step: (0,) * len(shape))


def column(height, wide, every=1, first=0):
    return pl.BlockSpec((height, wide), lambda step: (0, step * every + first))


def piece_of(layer, height, wide, first=0):
    return pl.BlockSpec((None, None, height, wide), lambda step: (layer, step, 0, first))


def slab(layer, height, wide):
    return pl.BlockSpec((None, height, wide), lambda step: (layer, 0, step))


def heads_of(layer):
    return pl.BlockSpec((None, None, HEADS, 3 * PAIR), lambda step: (step, layer, 0, 0))


def sheet(layer, height, wide):
    return pl.BlockSpec((None, height, wide), lambda step: (layer, 0, 0))


def shaped(shape, kind=BF16):
    return jax.ShapeDtypeStruct(shape, kind)


class Neighbours:
    def __init__(self):
        fsdp, tp = lax.axis_index("fsdp"), lax.axis_index("tp")
        self.size = lax.axis_size("tp")
        self.tp = tp
        self.x, self.y, self.core = ({"fsdp": jnp.bitwise_xor(fsdp, bit)} for bit in (2, 4, 1))

    def along(self, distance):
        return {"tp": lax.rem(self.tp + distance, self.size)}

    def all(self):
        return [self.x, self.y, self.core] + [self.along(distance) for distance in range(1, self.size)]

    def greet(self):
        targets = self.all()
        barrier = pltpu.get_barrier_semaphore()
        for target in targets:
            pl.semaphore_signal(barrier, inc=1, device_id=target, device_id_type=MESH)
        pl.semaphore_wait(barrier, len(targets))


class Plan:
    LINKS = {"x": (45.5e3, 1.5), "y": (45.5e3, 1.5), "z": (45.5e3, 2.2), "core": (600e3, 1.0)}

    def __init__(self):
        self.depth, self.clock = {"x": 5.0, "y": 5.0, "z": 5.0, "core": 20.0}, 0.0
        self.free, self.here, self.jobs, self.table = dict.fromkeys(self.LINKS, 0.0), {}, [], {}

    def add(self, rank, work, needs, copies, gives, group):
        self.jobs.append((rank, len(self.jobs), work, needs, copies, gives, group))
        self.jobs.sort(key=lambda job: job[:2])

    def carry(self, copies, gives):
        end = self.clock
        for link, size in copies:
            rate, latency = self.LINKS[link]
            self.free[link] = max(self.free[link], self.clock) + size / rate
            end = max(end, self.free[link] + latency)
        self.here[gives] = end

    def slot(self, *at):
        found = True
        while found:
            found = False
            for job in self.jobs:
                _, _, work, needs, copies, gives, _ = job
                ready = all(self.here.get(need, float("inf")) <= self.clock for need in needs)
                if ready and all(self.free[link] - self.clock < self.depth[link] for link, _ in copies):
                    self.carry(copies, gives)
                    self.table.setdefault(at, []).append(work)
                    self.jobs.remove(job)
                    found = True
                    break

    def wait(self, key, work, *at):
        self.slot(*at)
        while self.here.get(key, float("inf")) > self.clock:
            self.clock += 0.25
            self.slot(*at)
        self.table.setdefault(at, []).append(work)

    def finish(self, group, *at):
        self.slot(*at)
        while any(group in (None, job[-1]) for job in self.jobs):
            self.clock += 0.25
            self.slot(*at)

    def spend(self, time):
        self.clock += time


def turn(index, pieces):
    if isinstance(index, int):
        return (index + 1) // 2 if index % 2 else (pieces - index // 2) % pieces
    return jnp.where(lax.rem(index, 2) == 1, (index + 1) // 2, lax.rem(pieces - index // 2, pieces))


class Gather:
    KINDS = 7

    def __init__(self, peers, shard, near, far, send, recv, local, near_out, far_out, stored):
        self.peers, self.shard, self.near, self.far = peers, shard, near, far
        self.send, self.recv, self.local = send, recv, local
        self.outs, self.stored = (near_out, far_out), stored
        self.chunk, self.wide = shard.shape
        self.pieces = near.shape[0]

    def at(self, piece, start, count, half=None):
        first, wide = (0, self.wide) if half is None else (half * (self.wide // 2), self.wide // 2)
        return self.near.at[piece, pl.ds(start * self.chunk, count * self.chunk), pl.ds(first, wide)]

    def copy(self, piece, kind, source, target, device):
        return pltpu.make_async_remote_copy(
            src_ref=source, dst_ref=target, send_sem=self.send.at[piece, kind], recv_sem=self.recv.at[piece, kind],
            device_id=device, device_id_type=MESH,
        )

    def copies(self, piece, stage):
        if stage == "z":
            return [self.copy(piece, 0, self.shard, self.at(piece, 0, 1), self.peers.along(piece))] if piece else []
        if stage == "first":
            half = self.wide // 2
            left = self.shard.at[:, pl.ds(0, half)] if piece == 0 else self.at(piece, 0, 1, 0)
            right = self.shard.at[:, pl.ds(half, half)] if piece == 0 else self.at(piece, 0, 1, 1)
            return [
                self.copy(piece, 1, left, self.at(piece, 1, 1, 0), self.peers.x),
                self.copy(piece, 2, right, self.at(piece, 2, 1, 1), self.peers.y),
            ]
        if stage == "second":
            return [
                self.copy(piece, 3, self.at(piece, 0, 2, 0), self.at(piece, 2, 2, 0), self.peers.y),
                self.copy(piece, 4, self.at(piece, 0, 1, 1), self.at(piece, 1, 1, 1), self.peers.x),
                self.copy(piece, 5, self.at(piece, 2, 1, 1), self.at(piece, 3, 1, 1), self.peers.x),
            ]
        return [self.copy(piece, 6, self.near.at[piece], self.far.at[piece], self.peers.core)]

    def start(self, piece, stage):
        for copy in self.copies(piece, stage):
            copy.start()

    def arrived(self, piece, stage):
        for copy in self.copies(piece, stage):
            copy.wait_recv()

    def store(self, piece):
        return [
            pltpu.make_async_copy(source.at[piece], target.at[piece], self.stored.at[piece, which])
            for which, (source, target) in enumerate(zip((self.near, self.far), self.outs))
        ]

    def own(self):
        return pltpu.make_async_copy(self.shard, self.at(0, 0, 1), self.local)

    def sent(self, piece):
        self.start(piece, "z")

    def landed(self, piece):
        self.arrived(piece, "z")
        self.start(piece, "first")

    def crossed(self, piece):
        self.arrived(piece, "first")
        self.start(piece, "second")

    def shared(self, piece):
        self.arrived(piece, "second")
        self.start(piece, "core")

    def need(self, piece):
        self.arrived(piece, "core")
        for copy in self.store(piece):
            copy.start()

    def jobs(self, plan, index):
        size = self.chunk * self.wide * 2
        for place in range(self.pieces):
            piece = turn(place, self.pieces)
            key = (index, piece)
            rank = index * self.pieces + place
            if piece:
                plan.add(rank, (self.sent, piece), [], [("z", size * self.pieces / (self.pieces - 1))], ("z", *key), index)
            both = lambda count: [("x", count * size), ("y", count * size)]
            plan.add(rank, (self.landed, piece), [("z", *key)] if piece else [], both(0.5), ("first", *key), index)
            plan.add(rank, (self.crossed, piece), [("first", *key)], both(1), ("second", *key), index)
            plan.add(rank, (self.shared, piece), [("second", *key)], [("core", 4 * size)], ("core", *key), index)

    def end(self):
        for piece in range(self.pieces):
            for stage in ("z", "first", "second", "core"):
                for copy in self.copies(piece, stage):
                    copy.wait_send()
            for copy in self.store(piece):
                copy.wait()


class Halo:
    def __init__(self, ref, rows, send, recv):
        self.ref, self.send, self.recv = ref, send, recv
        self.place, self.size = lax.axis_index("tp"), lax.axis_size("tp")
        spill = REACH - rows
        self.moves = [
            (1, pl.ds(REACH, rows), pl.ds(spill, rows)),
            (-1, pl.ds(REACH, rows), pl.ds(REACH + rows, rows)),
            (2, pl.ds(2 * rows, spill), pl.ds(0, spill)),
            (-2, pl.ds(REACH, spill), pl.ds(REACH + 2 * rows, spill)),
        ]

    def inside(self, distance):
        other = self.place + distance
        return jnp.logical_and(other >= 0, other < self.size)

    def copy(self, index):
        distance, source, target = self.moves[index]
        return pltpu.make_async_remote_copy(
            src_ref=self.ref.at[source, :], dst_ref=self.ref.at[target, :], send_sem=self.send.at[index],
            recv_sem=self.recv.at[index], device_id={"tp": self.place + distance}, device_id_type=MESH,
        )

    def begin(self):
        for index, (distance, _, target) in enumerate(self.moves):

            @pl.when(self.inside(distance))
            def _():
                self.copy(index).start()

            @pl.when(jnp.logical_not(self.inside(-distance)))
            def _():
                self.ref[target, :] = jnp.zeros((target.size, self.ref.shape[1]), BF16)

    def end(self, _=None):
        for index, (distance, _, _) in enumerate(self.moves):

            @pl.when(self.inside(distance))
            def _():
                self.copy(index).wait_send()

            @pl.when(self.inside(-distance))
            def _():
                self.copy(index).wait_recv()


def params(collective, memory=None):
    return pltpu.CompilerParams(collective_id=collective, has_side_effects=True, vmem_limit_bytes=memory)


LN_GAIN, LN_BIAS, OUT_BIAS, LAST_BIAS, FEATS = (0, 1), (2, 3), 4, 5, 6
PROJ_BIAS, HEAD_GAIN, HEAD_BIAS, HEADS = (0, 1, 2), (3, 4), 5, 6


def line(ref, row, start=0, wide=None):
    return ref[pl.ds(row, 1), pl.ds(start, wide or ref.shape[1] - start)]


def attend_work(
    a_ref, near_ref, far_ref, heads_ref, feats_ref, x_ref, q_ref, kv_ref, q_hat_ref, k_hat_ref, q_scale_ref, k_scale_ref,
    p_ref, o_ref, mid_ref, m_ref, mask_ref, acc_ref, opening, closing, hook,
):
    rows = q_ref.shape[0]
    half = near_ref.shape[0]

    @pl.when(opening)
    def _():
        acc_ref[...] = jnp.zeros_like(acc_ref)

    tile = lambda row, which: line(heads_ref, row, which * PAIR, PAIR)
    bias, (q_gain, k_gain), q_shift = PROJ_BIAS, HEAD_GAIN, HEAD_BIAS
    near, distant = halves(a_ref[...])
    own, own_far = halves(a_ref[REACH : REACH + rows, :])
    kv = nn(near, near_ref[:, PAIR : 4 * PAIR]) + nn(distant, far_ref[:, PAIR : 4 * PAIR])
    kv += side(tile(bias[1], 0), tile(bias[2], 0), tile(bias[1], 1) + tile(bias[2], 2))
    q = side(
        nn(own, near_ref[:, :PAIR]) + nn(own_far, far_ref[:, :PAIR]),
        nn(own, near_ref[:, 4 * PAIR : 5 * PAIR]) + nn(own_far, far_ref[:, 4 * PAIR : 5 * PAIR]),
    ) + line(heads_ref, bias[0], 0, 2 * PAIR)
    q_hat, q_scale = head_norm(q)
    k_hat, k_scale = head_norm(side(kv[:, :PAIR], kv[:, 2 * PAIR :]))
    qn = (q_hat * line(heads_ref, q_gain, 0, 2 * PAIR) + line(heads_ref, q_shift, 0, 2 * PAIR)).astype(BF16)
    qn = side(qn[:, :PAIR], only(qn[:, PAIR:], 0))
    kn = (k_hat * line(heads_ref, k_gain, 0, 2 * PAIR)).astype(BF16)
    v = kv[:, PAIR:].astype(BF16)
    low = lax.broadcasted_iota(jnp.int32, (1, PAIR), 1) < HD
    first, second = kn[:, :PAIR], jnp.where(low, kn[:, PAIR:], v[:, PAIR:])
    values = v[:, :PAIR]
    q_ref[...] = qn
    kv_ref[...] = side(first, values, second)
    q_hat_ref[...] = q_hat.astype(BF16)
    k_hat_ref[...] = k_hat.astype(BF16)
    q_scale_ref[...] = q_scale.astype(BF16)
    k_scale_ref[...] = k_scale.astype(BF16)
    hook(1)
    values_t, second_t = values.T, second.T
    mixed = []
    for head in range(3):
        if head:
            hook(head + 1)
        keys = (first, first, second)[head]
        query = only(qn[:, PAIR * (head // 2) : PAIR * (head // 2 + 1)] * HD ** (-0.5), head % 2).astype(BF16)
        scores = nt(keys, query) + mask_ref[...]
        weights = jnp.exp(scores - jnp.max(scores, axis=0, keepdims=True))
        total = jnp.sum(weights, axis=0, keepdims=True)
        probs = (weights * (1.0 / total)).astype(BF16)
        p_ref[head] = probs
        mixed.append(nn((values_t[:HD], values_t[HD:], second_t[HD:])[head], probs))
    o = jnp.concatenate([jnp.zeros_like(mixed[2]), mixed[2], mixed[0], mixed[1]], axis=0).T.astype(BF16)
    o_ref[...] = o
    acc_ref[:, :half] += nt(o, near_ref[:, 4 * PAIR :])
    acc_ref[:, half:] += nt(o, far_ref[:, 4 * PAIR :])

    @pl.when(closing)
    def _():
        mid = x_ref[...] + (acc_ref[...] + line(feats_ref, OUT_BIAS))
        mid_ref[...] = mid
        hat, _ = row_norm(mid)
        m_ref[...] = (hat * line(feats_ref, LN_GAIN[1]) + line(feats_ref, LN_BIAS[1])).astype(BF16)


def mlp_work(
    m_ref, mid_ref, near_ref, far_ref, up_shift, feats_ref, act_ref, slope_ref, x2_ref, acc_ref, opening, closing, hook,
):
    half = near_ref.shape[0]
    wide = act_ref.shape[1]

    @pl.when(opening)
    def _():
        acc_ref[...] = jnp.zeros_like(acc_ref)

    near, distant = halves(m_ref[...])
    hidden = nn(near, near_ref[:, :wide]) + nn(distant, far_ref[:, :wide]) + up_shift
    hook(1)
    phi = 0.5 * (1.0 + lax.erf(hidden * ROOT_HALF))
    act = (hidden * phi).astype(BF16)
    act_ref[...] = act
    slope_ref[...] = (phi + hidden * jnp.exp(-0.5 * hidden * hidden) * INV_ROOT_TWO_PI).astype(BF16)
    acc_ref[:, :half] += nt(act, near_ref[:, wide:])
    acc_ref[:, half:] += nt(act, far_ref[:, wide:])

    @pl.when(closing)
    def _():
        x2_ref[...] = mid_ref[...] + (acc_ref[...] + line(feats_ref, LAST_BIAS))


def norm_rows(x, feats_ref):
    hat, _ = row_norm(x)
    return (hat * line(feats_ref, LN_GAIN[0]) + line(feats_ref, LN_BIAS[0])).astype(BF16)


def quiet(slot):
    pass


def attend_kernel(
    a_ref, near_ref, far_ref, heads_ref, feats_ref, x_ref, seg_k_ref, seg_q_ref, *rest
):
    step = pl.program_id(0)
    mask_ref = rest[-2]

    @pl.when(step == 0)
    def _():
        mask_ref[...] = jnp.where(seg_k_ref[...] == seg_q_ref[...], 0.0, FILL)

    attend_work(
        a_ref, near_ref, far_ref, heads_ref, feats_ref, x_ref, *rest, step == 0, step == pl.num_programs(0) - 1, quiet
    )


def attend_shapes(rows, window):
    return [
        (rows, 2 * PAIR), (window, 3 * PAIR), (rows, 2 * PAIR), (window, 2 * PAIR), (rows, 2 * PAIR), (window, 2 * PAIR),
    ]


def attend(a_win, near, far, heads, feats, x, seg_k, seg_q, layer):
    window, width = a_win.shape
    rows = x.shape[0]
    half = width // 2
    pieces = near.shape[1]
    outs = attend_shapes(rows, window)
    return pl.pallas_call(
        attend_kernel,
        grid=(pieces,),
        in_specs=[
            whole((window, width)), piece_of(0, half, 6 * PAIR), piece_of(0, half, 6 * PAIR), heads_of(layer), sheet(layer, FEATS, width),
            whole((rows, width)), whole((window, 1)), whole((1, rows)),
        ],
        out_specs=[column(*shape) for shape in outs]
        + [pl.BlockSpec((3, window, rows), lambda step: (step, 0, 0)), column(rows, 2 * PAIR)] + [whole((rows, width))] * 2,
        out_shape=[shaped((height, pieces * wide)) for height, wide in outs]
        + [shaped((3 * pieces, window, rows)), shaped((rows, pieces * 2 * PAIR)), shaped((rows, width), F32), shaped((rows, width))],
        scratch_shapes=[pltpu.VMEM((window, rows), F32), pltpu.VMEM((rows, width), F32)],
        name="attend",
    )(a_win, near, far, heads, feats, x, seg_k, seg_q)


def mlp_kernel(m_ref, mid_ref, near_ref, far_ref, up_shift_ref, feats_ref, *rest):
    step = pl.program_id(0)
    mlp_work(
        m_ref, mid_ref, near_ref, far_ref, up_shift_ref[...], feats_ref, *rest, step == 0, step == pl.num_programs(0) - 1, quiet
    )


def mlp(m, mid, near, far, up_shift, feats, layer):
    rows, width = mid.shape
    half = width // 2
    _, pieces, _, wide = up_shift.shape
    hidden = pieces * wide
    full = whole((rows, width))
    return pl.pallas_call(
        mlp_kernel,
        grid=(pieces,),
        in_specs=[
            full, full, piece_of(0, half, 2 * wide), piece_of(0, half, 2 * wide), piece_of(layer, 1, wide), sheet(layer, FEATS, width),
        ],
        out_specs=[column(rows, wide), column(rows, wide), full],
        out_shape=[shaped((rows, hidden)), shaped((rows, hidden)), shaped((rows, width), F32)],
        scratch_shapes=[pltpu.VMEM((rows, width), F32)],
        name="mlp",
    )(m, mid, near, far, up_shift, feats)


class Share:
    def __init__(self, peers, mine, landed, chunks, send, recv):
        self.peers, self.mine, self.landed, self.chunks, self.send, self.recv = peers, mine, landed, chunks, send, recv
        self.pieces, self.lines = landed.shape[0], mine.shape[0]

    def copy(self, index, source, target, device):
        return pltpu.make_async_remote_copy(
            src_ref=source, dst_ref=target, send_sem=self.send.at[index], recv_sem=self.recv.at[index], device_id=device,
            device_id_type=MESH,
        )

    def along(self):
        place = self.landed.at[self.peers.tp]
        return [self.copy(d - 1, self.mine, place, self.peers.along(d)) for d in range(1, self.pieces)]

    def across(self, stage):
        count = 1 << stage
        device = (self.peers.x, self.peers.y, self.peers.core)[stage]
        source, target = self.chunks.at[pl.ds(0, count)], self.chunks.at[pl.ds(count, count)]
        return self.copy(self.pieces - 1 + stage, source, target, device)

    def begin(self):
        for copy in self.along():
            copy.start()
        self.landed[self.peers.tp] = self.mine[...]

    def meet(self, fine):
        for copy in self.along():
            copy.wait_recv()
        row, col = (lax.broadcasted_iota(jnp.int32, (PAIR, PAIR), axis) for axis in range(2))
        total = 0.0
        for place in range(self.pieces):
            spread = jnp.logical_and(row < fine, col == row + place * fine)
            total += nn(self.landed[place], spread.astype(F32).astype(BF16))
        self.chunks[0] = total.astype(BF16)
        self.across(0).start()

    def spread(self, stage):
        self.across(stage - 1).wait_recv()
        self.across(stage).start()

    def end(self):
        self.across(2).wait_recv()
        for copy in self.along() + [self.across(stage) for stage in range(3)]:
            copy.wait_send()

    def chunk_of(self, fsdp):
        away = jnp.bitwise_xor(lax.axis_index("fsdp"), fsdp)
        return lax.rem(away, 2) * (self.chunks.shape[0] // 2) + away // 2

    def features(self, lines, width):
        chunk = width // self.chunks.shape[0]
        row, col = (lax.broadcasted_iota(jnp.int32, (2 * PAIR, width), axis) for axis in range(2))
        total = 0.0
        for place in range(0, self.chunks.shape[0], 2):
            lane = lax.rem(row, PAIR)
            spread = jnp.logical_and(lane < chunk, col == (place + row // PAIR) * chunk + lane)
            both = side(self.chunks[place, :lines, :], self.chunks[place + 1, :lines, :])
            total += nn(both, spread.astype(F32).astype(BF16))
        return total

    def owner(self, place):
        return lax.rem(self.peers.tp + self.pieces - place, self.pieces)

    def heads(self, place, start, chunk):
        owner = self.owner(place)
        rows = pl.ds(start, 16)
        both = side(self.chunks[self.chunk_of(2 * owner), rows, :], self.chunks[self.chunk_of(2 * owner + 1), rows, :])
        row, col = (lax.broadcasted_iota(jnp.int32, (2 * PAIR, 3 * PAIR), axis) for axis in range(2))
        lane = lax.rem(row, PAIR)
        feature = row // PAIR * chunk + lane
        last = jnp.logical_and(feature >= PAIR, col == feature + 3 * HD)
        spread = jnp.logical_and(lane < chunk, jnp.logical_or(col == feature, last))
        return nn(both, spread.astype(F32).astype(BF16))

    def hidden(self, start, layers, parts, fine):
        rows = pl.ds(start, 16)
        block = jnp.concatenate(
            [self.chunks[self.chunk_of(2 * self.owner(i // 2) + i % 2), rows, :] for i in range(2 * self.pieces)], axis=0
        )
        wide = self.pieces * parts * fine
        row, col = (lax.broadcasted_iota(jnp.int32, (PAIR, wide), axis) for axis in range(2))
        line_of = lax.broadcasted_iota(jnp.int32, (block.shape[0], 1), 0)
        total = 0.0
        for part in range(parts):
            target = row // fine * (parts * fine) + part * fine + lax.rem(row, fine)
            spread = jnp.logical_and(row < self.pieces * fine, col == target)
            here = nn(block, spread.astype(F32).astype(BF16))
            total += jnp.where(lax.rem(line_of, parts) == part, here, 0.0)
        row, col = (lax.broadcasted_iota(jnp.int32, (2 * self.pieces * layers, block.shape[0]), axis) for axis in range(2))
        group = jnp.logical_and(row // layers == col // 16, lax.rem(row, layers) == lax.rem(col, 16) // parts)
        return nn(group.astype(F32).astype(BF16), total.astype(BF16))


def forward_kernel(
    token_ref, hot_ref, share_ref, seg_k_ref, seg_q_ref, attn_shard_ref, mlp_shard_ref,
    q_ref, kv_ref, q_hat_ref, k_hat_ref, q_scale_ref, k_scale_ref, p_ref, o_ref, act_ref, slope_ref, mid_ref, m_ref, x2_ref,
    x0_ref, feats_ref, heads_ref, a_win_out, attn_near_out, attn_far_out, mlp_near_out, mlp_far_out,
    mask_ref, acc_ref, now_ref, a_win_ref, kept, attn_near, attn_far, mlp_near, mlp_far, send, recv, local, stored, halo_send, halo_recv,
    up_shift_ref, landed, chunks, share_send, share_recv,
):
    layers, pieces, (rows, width) = attn_near.shape[0], attn_near.shape[1], token_ref.shape
    chunk = width // chunks.shape[0]
    fine, parts, tables = chunk // pieces, act_ref.shape[1] * pieces // width, hot_ref.shape[1]
    step = pl.program_id(0)
    peers = Neighbours()
    halo = lambda layer: Halo(a_win_ref.at[layer], rows, halo_send.at[layer], halo_recv.at[layer])
    keep_window = lambda layer: pltpu.make_async_copy(a_win_ref.at[layer], a_win_out.at[layer], kept.at[layer])

    def window(layer):
        halo(layer).end()
        keep_window(layer).start()

    gathers = []
    for layer in range(layers):
        for which, (shard, near, far, near_out, far_out) in enumerate((
            (attn_shard_ref, attn_near, attn_far, attn_near_out, attn_far_out),
            (mlp_shard_ref, mlp_near, mlp_far, mlp_near_out, mlp_far_out),
        )):
            index = 2 * layer + which
            gathers.append(
                Gather(
                    peers, shard.at[layer], near.at[layer], far.at[layer], send.at[index], recv.at[index], local.at[index],
                    near_out.at[layer], far_out.at[layer], stored.at[index],
                )
            )

    share = Share(peers, share_ref, landed, chunks, share_send, share_recv)

    def open_up(_):
        share.end()
        lines = tables + 16
        found = share.features(lines, width)
        for layer in range(layers):
            feats_ref[layer] = found[tables + layer * FEATS : tables + (layer + 1) * FEATS]
        x0 = token_ref[...] + nn(hot_ref[...], found[:tables].astype(BF16))
        x0_ref[...] = x0
        now_ref[...] = x0
        a_win_ref[0, REACH : REACH + rows, :] = norm_rows(x0, feats_ref.at[0])
        halo(0).begin()
        for piece in range(pieces):
            found = share.heads(piece, lines, chunk)
            for layer in range(layers):
                heads_ref[piece, layer] = found[layer * HEADS : (layer + 1) * HEADS]
        found = share.hidden(lines + 16, layers, parts, fine)
        half = pieces * parts * fine
        for index in range(2 * pieces):
            for layer in range(layers):
                at = index * layers + layer
                up_shift_ref[layer, index // 2, :, index % 2 * half : (index % 2 + 1) * half] = found[at : at + 1]

    plan = Plan()
    for index, gather in enumerate(gathers):
        gather.jobs(plan, index)
    halo_size = width * 2 * 2 * rows
    share_size = share_ref.shape[0] * PAIR * 2
    plan.spend(2.5)
    plan.carry([("z", pieces * share_size)], ("share", 0))
    plan.wait(("share", 0), (share.meet, fine), 0, 0)
    plan.carry([("x", share_size)], ("share", 1))
    plan.wait(("share", 1), (share.spread, 1), 0, 0)
    plan.carry([("y", 2 * share_size)], ("share", 2))
    plan.wait(("share", 2), (share.spread, 2), 0, 0)
    plan.carry([("core", 4 * share_size)], ("share", 3))
    plan.wait(("share", 3), (open_up, 0), 0, 0)
    for layer in range(layers):
        plan.carry([("z", halo_size)], ("halo", layer))
        first = 1 + 2 * layer * pieces
        if layer == 0:
            plan.spend(5.0)
        plan.wait(("halo", layer), (window, layer), *((first, 0) if layer else (0, 0)))
        for index in range(pieces):
            piece = turn(index, pieces)
            plan.wait(("core", 2 * layer, piece), (gathers[2 * layer].need, piece), first + index, 0)
            for slot, time in enumerate((2.0, 1.4, 1.4)):
                plan.spend(time)
                plan.slot(first + index, slot + 1)
            plan.spend(1.4)
        first += pieces
        for index in range(pieces):
            piece = turn(index, pieces)
            plan.wait(("core", 2 * layer + 1, piece), (gathers[2 * layer + 1].need, piece), first + index, 0)
            plan.spend(1.0)
            plan.slot(first + index, 1)
            plan.spend(1.5)
    table = plan.table

    def run(at, slot):
        if (at, slot) in table:

            @pl.when(step == at)
            def _():
                for work, piece in table[at, slot]:
                    work(piece)

    @pl.when(step == 0)
    def _():
        peers.greet()
        mask_ref[...] = jnp.where(seg_k_ref[...] == seg_q_ref[...], 0.0, FILL)
        share.begin()
        for gather in gathers:
            gather.own().start()
        for gather in gathers:
            gather.own().wait()

    run(0, 0)

    count = jnp.maximum(step - 1, 0)
    layer = count // (2 * pieces)
    inner = lax.rem(count, 2 * pieces)
    index = lax.rem(inner, pieces)
    piece = turn(index, pieces)
    steps_of = lambda which: [
        1 + (2 * layer + which) * pieces + index for layer in range(layers) for index in range(pieces)
    ]

    @pl.when(jnp.logical_and(step > 0, inner < pieces))
    def _():
        def hook(slot):
            for at in steps_of(0):
                run(at, slot)

        hook(0)
        attend_work(
            a_win_ref.at[layer], attn_near.at[layer, piece], attn_far.at[layer, piece], heads_ref.at[piece, layer],
            feats_ref.at[layer], now_ref,
            q_ref, kv_ref, q_hat_ref, k_hat_ref, q_scale_ref, k_scale_ref, p_ref, o_ref, mid_ref.at[layer], m_ref.at[layer],
            mask_ref, acc_ref, index == 0, index == pieces - 1, hook,
        )

    @pl.when(inner >= pieces)
    def _():
        def hook(slot):
            for at in steps_of(1):
                run(at, slot)

        hook(0)
        mlp_work(
            m_ref.at[layer], mid_ref.at[layer], mlp_near.at[layer, piece], mlp_far.at[layer, piece],
            up_shift_ref[layer, piece], feats_ref.at[layer], act_ref, slope_ref, now_ref, acc_ref, index == 0,
            index == pieces - 1, hook,
        )

        @pl.when(index == pieces - 1)
        def _():
            x2_ref[layer] = now_ref[...]

            @pl.when(layer + 1 < layers)
            def _():
                a_win_ref[layer + 1, REACH : REACH + rows, :] = norm_rows(now_ref[...], feats_ref.at[layer + 1])
                halo(layer + 1).begin()

    @pl.when(step == pl.num_programs(0) - 1)
    def _():
        for gather in gathers:
            gather.end()
        for layer in range(layers):
            keep_window(layer).wait()


def forward(tokens, hot, share, seg_k, seg_q, attn_shards, mlp_shards):
    rows, width = tokens.shape
    layers, chunk, wide = mlp_shards.shape
    half = width // 2
    window = rows + 2 * REACH
    pieces, chunks, part = lax.axis_size("tp"), lax.axis_size("fsdp"), wide // 2
    hidden = pieces * part

    def attend_at(step):
        count = jnp.maximum(step - 1, 0)
        layer, inner = count // (2 * pieces), lax.rem(count, 2 * pieces)
        return layer, turn(jnp.minimum(inner, pieces - 1), pieces)

    def mlp_at(step):
        count = jnp.maximum(step - 1, 0)
        layer, inner = count // (2 * pieces), lax.rem(count, 2 * pieces)
        done = jnp.where(inner >= pieces, layer * pieces + inner - pieces, jnp.maximum(layer * pieces - 1, 0))
        return done // pieces, turn(lax.rem(done, pieces), pieces)

    def attend_block(height, wide):
        return pl.BlockSpec((None, height, wide), lambda step: (attend_at(step)[0], 0, attend_at(step)[1]))

    mlp_block = pl.BlockSpec((None, rows, part), lambda step: (mlp_at(step)[0], 0, mlp_at(step)[1]))
    heads_at = lambda step: attend_at(step)[0] * pieces + attend_at(step)[1]
    once = lambda shape: pl.BlockSpec(shape, lambda step: (0,) * len(shape), pipeline_mode=pl.Buffered(1))
    outs = attend_shapes(rows, window) + [(rows, 2 * PAIR)]
    specs = [attend_block(*shape) for shape in outs]
    shapes = [shaped((layers, height, pieces * wide)) for height, wide in outs]
    specs.insert(6, pl.BlockSpec((3, window, rows), lambda step: (heads_at(step), 0, 0)))
    shapes.insert(6, shaped((3 * layers * pieces, window, rows)))
    held = [((layers, rows, width), F32), ((layers, rows, width), BF16), ((layers, rows, width), F32)]
    weights = [(layers, pieces, half, 6 * PAIR)] * 2 + [(layers, pieces, half, wide)] * 2
    semaphores = pltpu.SemaphoreType.DMA((2 * layers, pieces, Gather.KINDS))
    held += [((rows, width), F32), ((layers, FEATS, width), F32), ((pieces, layers, HEADS, 3 * PAIR), F32)]
    inputs = (tokens, hot, share, seg_k, seg_q, attn_shards, mlp_shards)
    return pl.pallas_call(
        forward_kernel,
        grid=(1 + 2 * layers * pieces,),
        in_specs=[once(item.shape) for item in inputs],
        out_specs=specs + [mlp_block] * 2 + [once(shape) for shape, _ in held] + [ANY] * 5,
        out_shape=shapes + [shaped((layers, rows, hidden))] * 2 + [shaped(*item) for item in held]
        + [shaped(shape) for shape in [(layers, window, width)] + weights],
        scratch_shapes=[
            pltpu.VMEM((window, rows), F32), pltpu.VMEM((rows, width), F32), pltpu.VMEM((rows, width), F32),
            pltpu.VMEM((layers, window, width), BF16), pltpu.SemaphoreType.DMA((layers,)),
            *[pltpu.VMEM(shape, BF16) for shape in weights], semaphores, semaphores, pltpu.SemaphoreType.DMA((2 * layers,)),
            pltpu.SemaphoreType.DMA((2 * layers, pieces, 2)), pltpu.SemaphoreType.DMA((layers, 4)),
            pltpu.SemaphoreType.DMA((layers, 4)), pltpu.VMEM((layers, pieces, 1, part), F32),
            pltpu.VMEM((pieces, *share.shape), BF16), pltpu.VMEM((chunks, *share.shape), BF16),
            pltpu.SemaphoreType.DMA((pieces + 2,)), pltpu.SemaphoreType.DMA((pieces + 2,)),
        ],
        compiler_params=params(20, VMEM),
        name="forward",
    )(*inputs)


def mlp_back_kernel(*refs):
    step = pl.program_id(0)
    mlp_back_work(*refs, step == 0, step == pl.num_programs(0) - 1, quiet)


def mlp_back_work(
    g_ref, down_near_ref, down_far_ref, slope_ref, up_near_ref, up_far_ref, mid_ref, feats_ref,
    gz_ref, gh_ref, up_shift_grad_ref, g1_ref, gr_ref, small_ref, acc_ref, opening, closing, hook,
):
    half = up_near_ref.shape[0]

    @pl.when(opening)
    def _():
        gz_ref[...] = g_ref[...].astype(BF16)
        acc_ref[...] = jnp.zeros_like(acc_ref)

    near, distant = halves(gz_ref[...])
    gh = ((nn(near, down_near_ref[...]) + nn(distant, down_far_ref[...])) * slope_ref[...].astype(F32)).astype(BF16)
    gh_ref[...] = gh
    hook(1)
    up_shift_grad_ref[...] = jnp.sum(gh.astype(F32), axis=0, keepdims=True)
    acc_ref[:, :half] += nt(gh, up_near_ref[...])
    acc_ref[:, half:] += nt(gh, up_far_ref[...])

    @pl.when(closing)
    def _():
        gm = acc_ref[...]
        hat, scale = row_norm(mid_ref[...])
        g1 = g_ref[...] + row_norm_back(gm * line(feats_ref, LN_GAIN[1]), hat, scale)
        gr = g1.astype(BF16)
        g1_ref[...] = g1
        gr_ref[...] = gr
        small_ref[...] = jnp.zeros_like(small_ref)
        small_ref[0:1, :] = jnp.sum(gz_ref[...].astype(F32), axis=0, keepdims=True)
        small_ref[1:2, :] = jnp.sum(gr.astype(F32), axis=0, keepdims=True)
        small_ref[2:3, :] = jnp.sum(gm * hat, axis=0, keepdims=True)
        small_ref[3:4, :] = jnp.sum(gm, axis=0, keepdims=True)


def mlp_back(grad, near, far, slope, mid, feats, layer, index):
    rows, width = grad.shape
    half = width // 2
    hidden = slope.shape[2]
    pieces = near.shape[1]
    wide = hidden // pieces
    full = whole((rows, width))
    return pl.pallas_call(
        mlp_back_kernel,
        grid=(pieces,),
        in_specs=[
            full, piece_of(index, half, wide, 1), piece_of(index, half, wide, 1), slab(index, rows, wide),
            piece_of(index, half, wide), piece_of(index, half, wide), sheet(index, rows, width), sheet(layer, FEATS, width),
        ],
        out_specs=[full, column(rows, wide), column(1, wide), full, full, whole((8, width))],
        out_shape=[
            shaped((rows, width)), shaped((rows, hidden)), shaped((1, hidden), F32), shaped((rows, width), F32),
            shaped((rows, width)), shaped((8, width), F32),
        ],
        scratch_shapes=[pltpu.VMEM((rows, width), F32)],
        cost_estimate=pl.CostEstimate(
            flops=4 * rows * width * hidden, bytes_accessed=4 * width * hidden, transcendentals=0
        ),
        name="mlp_back",
    )(grad, near, far, slope, near, far, mid, feats)


def attend_back_kernel(*refs):
    *ins, gq_ref, gkv_ref, mine_ref, left_ref, right_ref, small_ref, acc_ref = refs
    rows = gq_ref.shape[0]
    step = pl.program_id(0)

    @pl.when(step == 0)
    def _():
        acc_ref[...] = jnp.zeros_like(acc_ref)

    attend_back_work(*ins, gq_ref, gkv_ref, small_ref, acc_ref, quiet)

    @pl.when(step == pl.num_programs(0) - 1)
    def _():
        left_ref[...] = acc_ref[:REACH, :].astype(BF16)
        mine_ref[...] = acc_ref[REACH : REACH + rows, :]
        right_ref[...] = acc_ref[REACH + rows :, :].astype(BF16)


def attend_back_work(
    gr_ref, q_ref, kv_ref, q_hat_ref, k_hat_ref, q_scale_ref, k_scale_ref, p_ref, near_ref, far_ref, heads_ref,
    gq_ref, gkv_ref, small_ref, acc_ref, hook,
):
    rows = gr_ref.shape[0]
    half = near_ref.shape[0]
    near, distant = halves(gr_ref[...])
    go = (nn(near, near_ref[:, 4 * PAIR :]) + nn(distant, far_ref[:, 4 * PAIR :])).astype(BF16)
    qn, kv = q_ref[...], kv_ref[...]
    first, values, second = kv[:, :PAIR], kv[:, PAIR : 2 * PAIR], kv[:, 2 * PAIR :]
    first_t, second_t = first.T, second.T
    grad_q, grad_k, grad_v = [], [], []
    for head in range(3):
        if head:
            hook(head)
        go_head = only(go[:, PAIR:], head) if head < 2 else only(go[:, :PAIR], 1)
        query = only(qn[:, PAIR * (head // 2) : PAIR * (head // 2 + 1)] * HD ** (-0.5), head % 2).astype(BF16)
        stored = p_ref[head]
        probs = stored.astype(F32)
        grad_probs = nt((values, values, second)[head], go_head)
        delta = jnp.sum(probs * grad_probs, axis=0, keepdims=True)
        grad_scores = (probs * (grad_probs - delta)).astype(BF16)
        grad_v.append(nn(stored, go_head))
        grad_k.append(nn(grad_scores, query))
        grad_q.append(nn((first_t[:HD], first_t[HD:], second_t[:HD])[head], grad_scores))
    hook(3)
    zero = jnp.zeros_like(grad_q[2])
    grad_q = (jnp.concatenate(grad_q + [zero], axis=0) * HD ** (-0.5)).T
    grad_k = side(grad_k[0] + grad_k[1], grad_k[2])
    pair_v, last_v = grad_v[0] + grad_v[1], grad_v[2]
    q_hat = q_hat_ref[...].astype(F32)
    k_hat = k_hat_ref[...].astype(F32)
    gain = lambda which: line(heads_ref, HEAD_GAIN[which], 0, 2 * PAIR)
    gq = head_norm_back(grad_q * gain(0), q_hat, q_scale_ref[...].astype(F32)).astype(BF16)
    gk = head_norm_back(grad_k * gain(1), k_hat, k_scale_ref[...].astype(F32)).astype(BF16)
    gkv = side(gk[:, :PAIR], pair_v.astype(BF16), gk[:, PAIR:] + last_v.astype(BF16))
    gq_ref[...] = gq
    gkv_ref[...] = gkv
    total = lambda value: jnp.sum(value.astype(F32), axis=0, keepdims=True)
    small_ref[...] = jnp.zeros_like(small_ref)
    small_ref[0:1, : 2 * PAIR] = total(grad_q * q_hat)
    small_ref[1:2, : 2 * PAIR] = total(grad_k * k_hat)
    small_ref[2:3, : 2 * PAIR] = total(grad_q)
    small_ref[3:4, : 2 * PAIR] = total(gq)
    small_ref[4:5, : 2 * PAIR] = total(gk)
    small_ref[5:6, :PAIR] = total(pair_v.astype(BF16))
    small_ref[5:6, 2 * PAIR :] = total(last_v.astype(BF16))
    acc_ref[:, :half] += nt(gkv, near_ref[:, PAIR : 4 * PAIR])
    acc_ref[:, half:] += nt(gkv, far_ref[:, PAIR : 4 * PAIR])
    own = slice(REACH, REACH + rows)
    for ref, cols in ((near_ref, slice(0, half)), (far_ref, slice(half, 2 * half))):
        acc_ref[own, cols] += nt(gq[:, :PAIR], ref[:, :PAIR]) + nt(gq[:, PAIR:], ref[:, 4 * PAIR : 5 * PAIR])


def attend_back_specs(rows, width, pieces, layer, index):
    half = width // 2
    window = rows + 2 * REACH
    full = whole((rows, width))
    in_specs = [
        full, *[slab(index, *shape) for shape in attend_shapes(rows, window)],
        pl.BlockSpec((3, window, rows), lambda step: (index * pieces + step, 0, 0)), piece_of(index, half, 6 * PAIR),
        piece_of(index, half, 6 * PAIR), heads_of(layer),
    ]
    out_specs = [
        column(rows, 2 * PAIR), column(window, 3 * PAIR), full, whole((REACH, width)), whole((REACH, width)), column(8, 3 * PAIR),
    ]
    out_shape = [
        shaped((rows, pieces * 2 * PAIR)), shaped((window, pieces * 3 * PAIR)), shaped((rows, width), F32),
        shaped((REACH, width)), shaped((REACH, width)), shaped((8, pieces * 3 * PAIR), F32),
    ]
    cost = pl.CostEstimate(
        flops=2 * window * width * width * 2 + 20 * window * rows * width * 2,
        bytes_accessed=20 * window * width,
        transcendentals=0,
    )
    return in_specs, out_specs, out_shape, [pltpu.VMEM((window, width), F32)], cost


def attend_back(gr, stored, near, far, heads, layer, index):
    rows, width = gr.shape
    pieces = near.shape[1]
    in_specs, out_specs, out_shape, scratch, cost = attend_back_specs(rows, width, pieces, layer, index)
    return pl.pallas_call(
        attend_back_kernel,
        grid=(pieces,),
        in_specs=in_specs,
        out_specs=out_specs,
        out_shape=out_shape,
        scratch_shapes=scratch,
        cost_estimate=cost,
        name="attend_back",
    )(gr, *stored, near, far, heads)


def attn_weight_kernel(a_ref, gq_ref, gkv_ref, gr_ref, o_ref, keep_ref, send_ref, a_t_ref, gr_t_ref):
    rows = gq_ref.shape[0]
    half = keep_ref.shape[0]

    @pl.when(pl.program_id(0) == 0)
    def _():
        a_t_ref[...] = a_ref[...].T
        gr_t_ref[...] = gr_ref[...].T

    for part, ref in ((slice(0, half), keep_ref), (slice(half, 2 * half), send_ref)):
        from_q = nn(a_t_ref[part, REACH : REACH + rows], gq_ref[...])
        from_o = nn(gr_t_ref[part, :], o_ref[...])
        ref[:, :PAIR] = from_q[:, :PAIR].astype(BF16)
        ref[:, PAIR : 4 * PAIR] = nn(a_t_ref[part, :], gkv_ref[...]).astype(BF16)
        ref[:, 4 * PAIR : 5 * PAIR] = (from_q[:, PAIR:] + from_o[:, :PAIR]).astype(BF16)
        ref[:, 5 * PAIR :] = from_o[:, PAIR:].astype(BF16)


def attn_weight_grads(a_win, gq, gkv, gr, o):
    _, window, width = a_win.shape
    rows = gr.shape[0]
    half = width // 2
    pieces = gq.shape[1] // (2 * PAIR)
    out = column(half, 6 * PAIR)
    return pl.pallas_call(
        attn_weight_kernel,
        grid=(pieces,),
        in_specs=[
            sheet(0, window, width), column(rows, 2 * PAIR), column(window, 3 * PAIR), whole((rows, width)),
            slab(0, rows, 2 * PAIR),
        ],
        out_specs=[out, out],
        out_shape=[shaped((half, pieces * 6 * PAIR))] * 2,
        scratch_shapes=[pltpu.VMEM((width, window), BF16), pltpu.VMEM((width, rows), BF16)],
        cost_estimate=pl.CostEstimate(
            flops=2 * width * width * (2 * window + 2 * rows), bytes_accessed=8 * width * width, transcendentals=0
        ),
        name="attn_weight_grads",
    )(a_win, gq, gkv, gr, o)


def mlp_weight_kernel(m_ref, gh_ref, gz_ref, act_ref, keep_ref, send_ref, m_t_ref, gz_t_ref):
    half = keep_ref.shape[0]
    wide = gh_ref.shape[1]

    @pl.when(pl.program_id(0) == 0)
    def _():
        m_t_ref[...] = m_ref[...].T
        gz_t_ref[...] = gz_ref[...].T

    for part, ref in ((slice(0, half), keep_ref), (slice(half, 2 * half), send_ref)):
        ref[:, :wide] = nn(m_t_ref[part, :], gh_ref[...]).astype(BF16)
        ref[:, wide:] = nn(gz_t_ref[part, :], act_ref[...]).astype(BF16)


def mlp_weight_grads(m, gh, gz, act):
    _, rows, width = m.shape
    half = width // 2
    hidden = gh.shape[1]
    pieces = lax.axis_size("tp")
    wide = hidden // pieces
    out = column(half, 2 * wide)
    return pl.pallas_call(
        mlp_weight_kernel,
        grid=(pieces,),
        in_specs=[sheet(0, rows, width), column(rows, wide), whole((rows, width)), slab(0, rows, wide)],
        out_specs=[out, out],
        out_shape=[shaped((half, 2 * hidden))] * 2,
        scratch_shapes=[pltpu.VMEM((width, rows), BF16), pltpu.VMEM((width, rows), BF16)],
        cost_estimate=pl.CostEstimate(
            flops=4 * width * hidden * rows, bytes_accessed=4 * width * hidden, transcendentals=0
        ),
        name="mlp_weight_grads",
    )(m, gh, gz, act)


class Scatter:
    KINDS = 7

    def __init__(self, peers, out, away, keep, core, first, second, given, send, recv):
        self.peers, self.out, self.away, self.keep, self.core_in = peers, out, away, keep, core
        self.first_in, self.second_in, self.given, self.send, self.recv = first, second, given, send, recv
        self.chunk, self.wide = out.shape
        self.half = self.wide // 2
        self.pieces = keep.shape[0]

    def copy(self, piece, kind, source, target, device):
        return pltpu.make_async_remote_copy(
            src_ref=source, dst_ref=target, send_sem=self.send.at[piece, kind], recv_sem=self.recv.at[piece, kind],
            device_id=device, device_id_type=MESH,
        )

    def copies(self, piece, stage):
        c, left, right = self.chunk, pl.ds(0, self.half), pl.ds(self.half, self.half)
        rows = lambda start, count=1: pl.ds(start * c, count * c)
        if stage == "core":
            return [self.copy(piece, 0, self.away.at[self.slot(piece)], self.core_in.at[piece], self.peers.core)]
        if stage == "first":
            source, target = self.keep.at[piece], self.first_in.at[piece]
            return [
                self.copy(piece, 1, source.at[rows(2, 2), left], target.at[:, left], self.peers.y),
                self.copy(piece, 2, source.at[rows(1), right], target.at[rows(0), right], self.peers.x),
                self.copy(piece, 3, source.at[rows(3), right], target.at[rows(1), right], self.peers.x),
            ]
        if stage == "second":
            source, target = self.keep.at[piece], self.second_in.at[piece]
            return [
                self.copy(piece, 4, source.at[rows(1), left], target.at[:, left], self.peers.x),
                self.copy(piece, 5, source.at[rows(2), right], target.at[:, right], self.peers.y),
            ]
        target = self.given.at[(piece - 1) % self.pieces]
        return [self.copy(piece, 6, self.keep.at[piece, rows(0), :], target, self.peers.along(1))]

    def start(self, piece, stage):
        for copy in self.copies(piece, stage):
            copy.start()

    def arrived(self, piece, stage):
        for copy in self.copies(piece, stage):
            copy.wait_recv()

    def add(self, piece, start, count, cols, source):
        step = 32

        @pl.loop(0, count * self.chunk // step)
        def _(index):
            row = pl.multiple_of(index * step, step)
            into = (piece, pl.ds(start * self.chunk + row, step), cols)
            self.keep[into] = self.keep[into] + source[pl.ds(row, step), cols]

    def slot(self, piece):
        return (piece + self.pieces - 1) % self.pieces % 2

    def room(self, index, piece):
        @pl.when(index > 1)
        def _():
            for copy in self.copies(lax.rem(piece + self.pieces - 2, self.pieces), "core"):
                copy.wait_send()

    def first(self, piece):
        self.arrived(piece, "core")
        self.add(piece, 0, 4, pl.ds(0, self.wide), self.core_in.at[piece])
        self.start(piece, "first")

    def second(self, piece):
        left, right = pl.ds(0, self.half), pl.ds(self.half, self.half)
        self.arrived(piece, "first")
        source = self.first_in.at[piece]
        self.add(piece, 0, 2, left, source)
        self.add(piece, 0, 1, right, source)
        self.add(piece, 2, 1, right, source.at[pl.ds(self.chunk, self.chunk)])
        self.start(piece, "second")

    def last(self, piece):
        self.arrived(piece, "second")
        kept = pl.ds(0, self.chunk)
        total = self.keep[piece, kept, :].astype(F32) + self.second_in[piece].astype(F32)
        if piece != 1:
            self.arrived((piece - 1) % self.pieces, "give")
            total += self.given[(piece - 2) % self.pieces].astype(F32)
        if piece:
            self.keep[piece, kept, :] = total.astype(BF16)
            self.start(piece, "give")
        else:
            self.out[...] = total

    def done(self):
        for piece in range(self.pieces):
            for stage in ("core", "first", "second", "give"):
                if (stage != "give" or piece) and (stage != "core" or piece in (0, self.pieces - 1)):
                    for copy in self.copies(piece, stage):
                        copy.wait_send()

    def made(self, plan, index, piece):
        size = self.chunk * self.wide * 2
        both = lambda count: [("x", count * size), ("y", count * size)]
        key = (index, piece)
        rank = index * self.pieces + (piece - 1) % self.pieces
        plan.carry([("core", 4 * size)], ("core", *key))
        plan.add(rank, (self.first, piece), [("core", *key)], both(1), ("first", *key), index)
        plan.add(rank, (self.second, piece), [("first", *key)], both(0.5), ("second", *key), index)
        needs = [("second", *key)] + ([("give", index, (piece - 1) % self.pieces)] if piece != 1 else [])
        plan.add(rank, (self.last, piece), needs, [("z", size)] if piece else [], ("give", *key), index)


class Return:
    def __init__(self, edges, landed, rows, send, recv):
        self.edges, self.landed, self.send, self.recv = edges, landed, send, recv
        self.place, self.size = lax.axis_index("tp"), lax.axis_size("tp")
        spill = REACH - rows
        self.moves = [
            (1, 1, pl.ds(0, rows), pl.ds(0, rows), 0),
            (-1, 0, pl.ds(spill, rows), pl.ds(rows, rows), 0),
            (2, 1, pl.ds(rows, spill), pl.ds(2 * rows, spill), 0),
            (-2, 0, pl.ds(0, spill), pl.ds(2 * rows + spill, spill), rows - spill),
        ]

    def inside(self, distance):
        other = self.place + distance
        return jnp.logical_and(other >= 0, other < self.size)

    def copy(self, index):
        distance, which, source, target, _ = self.moves[index]
        return pltpu.make_async_remote_copy(
            src_ref=self.edges.at[pl.ds(which * REACH + source.start, source.size), pl.ds(0, self.landed.shape[1])],
            dst_ref=self.landed.at[target, :], send_sem=self.send.at[index],
            recv_sem=self.recv.at[index], device_id={"tp": self.place + distance}, device_id_type=MESH,
        )

    def begin(self):
        for index, (distance, *_) in enumerate(self.moves):

            @pl.when(self.inside(distance))
            def _():
                self.copy(index).start()

    def end(self, total_ref):
        for index, (distance, _, _, target, start) in enumerate(self.moves):

            @pl.when(self.inside(distance))
            def _():
                self.copy(index).wait_send()

            @pl.when(self.inside(-distance))
            def _():
                self.copy(index).wait_recv()
                total_ref[pl.ds(start, target.size), :] += self.landed[target, :].astype(F32)


def split_dot(left, right):
    if left.dtype == F32:
        high = left.astype(BF16)
        return nn(high, right) + nn((left - high.astype(F32)).astype(BF16), right)
    high = right.astype(BF16)
    return nn(left, high) + nn(left, (right - high.astype(F32)).astype(BF16))


def picked(mask):
    return mask.astype(F32).astype(BF16)


class Tally:
    def __init__(self, peers, chunks, inbox, send, recv, pieces):
        self.peers, self.chunks, self.inbox, self.send, self.recv, self.pieces = peers, chunks, inbox, send, recv, pieces
        self.share = Share(peers, chunks.at[0], inbox.at[pl.ds(0, pieces)], chunks, send, recv)

    def across(self, stage):
        count = 4 >> stage
        device = (self.peers.core, self.peers.y, self.peers.x)[stage]
        source, target = self.chunks.at[pl.ds(count, count)], self.inbox.at[pl.ds(8 - 2 * count, count)]
        return self.share.copy(stage, source, target, device)

    def along(self):
        place = self.inbox.at[7 + self.peers.tp]
        return [self.share.copy(2 + d, self.chunks.at[0], place, self.peers.along(d)) for d in range(1, self.pieces)]

    def build(self, tables, lines_ref, work_ref, norm_sums, mlp_sums, head_sums, up_grad):
        layers, width = norm_sums.shape[0], lines_ref.shape[1]
        count = self.chunks.shape[0]
        chunk, first = width // count, tables.shape[0]
        fine, parts = chunk // self.pieces, up_grad.shape[3] * self.pieces // width
        lines_ref[:first, :] = tables
        lines_ref[first : first + 16, :] = jnp.zeros((16, width), F32)
        for layer in range(layers):
            sums = [(norm_sums, 0), (mlp_sums, 2), (norm_sums, 1), (mlp_sums, 3), (mlp_sums, 1), (mlp_sums, 0)]
            for index, (ref, row) in enumerate(sums):
                at = first + layer * FEATS + index
                lines_ref[at : at + 1, :] = ref[layer, row : row + 1, :]
        lines = lines_ref[: first + 16, :]
        row, col = (lax.broadcasted_iota(jnp.int32, (width, PAIR), axis) for axis in range(2))
        for place in range(count):
            spread = picked(jnp.logical_and(col < chunk, row == place * chunk + col))
            self.chunks[place, : first + 16, :] = split_dot(lines, spread).astype(BF16)
        row, col = (lax.broadcasted_iota(jnp.int32, (3 * PAIR, 2 * PAIR), axis) for axis in range(2))
        lane = lax.rem(col, PAIR)
        feature = col // PAIR * chunk + lane
        last = jnp.logical_and(feature >= PAIR, row == feature + 3 * HD)
        spread = picked(jnp.logical_and(lane < chunk, jnp.logical_or(row == feature, last)))
        work_ref[:32, :] = jnp.zeros((32, width), F32)
        for piece in range(self.pieces):
            for layer in range(layers):
                for index, line_at in enumerate((3, 4, 5, 0, 1, 2)):
                    at = layer * HEADS + index
                    work_ref[at : at + 1, : 3 * PAIR] = head_sums[layer, piece, line_at : line_at + 1, :]
            both = split_dot(work_ref[:16, : 3 * PAIR], spread).astype(BF16)
            owner = self.share.owner(piece)
            for index in range(2):
                target = self.chunks.at[self.share.chunk_of(2 * owner + index)]
                target[first + 16 : first + 32, :] = both[:, index * PAIR : (index + 1) * PAIR]
        wide = self.pieces * parts * fine
        for index in range(2 * self.pieces):
            for layer in range(layers):
                at = 16 + index * layers + layer
                half = slice(index % 2 * wide, (index % 2 + 1) * wide)
                work_ref[at : at + 1, :wide] = up_grad[layer, index // 2, :, half]
        biases = work_ref[16 : 16 + 2 * self.pieces * layers, :wide]
        row, col = (lax.broadcasted_iota(jnp.int32, (wide, PAIR), axis) for axis in range(2))
        shape = (2 * self.pieces * 16, 2 * self.pieces * layers)
        line_of, from_of = (lax.broadcasted_iota(jnp.int32, shape, axis) for axis in range(2))
        total = 0.0
        for part in range(parts):
            source = col // fine * (parts * fine) + part * fine + lax.rem(col, fine)
            here = split_dot(biases, picked(jnp.logical_and(col < chunk, row == source)))
            group = jnp.logical_and(line_of // 16 == from_of // layers, lax.rem(line_of, 16) == lax.rem(from_of, layers) * parts + part)
            total += split_dot(picked(group), here)
        for index in range(2 * self.pieces):
            target = self.chunks.at[self.share.chunk_of(2 * self.share.owner(index // 2) + index % 2)]
            target[first + 32 : first + 48, :] = total[index * 16 : (index + 1) * 16].astype(BF16)
        self.across(0).start()

    def fold(self, stage):
        count = 4 >> stage
        self.across(stage).wait_recv()
        mine, found = self.chunks[:count], self.inbox[8 - 2 * count : 8 - count]
        self.chunks[:count] = (mine.astype(F32) + found.astype(F32)).astype(BF16)
        if stage < 2:
            self.across(stage + 1).start()
        else:
            for copy in self.along():
                copy.start()

    def total(self, out_ref):
        total = self.chunks[0].astype(F32)
        for copy in self.along():
            copy.wait_recv()
        for distance in range(1, self.pieces):
            total += self.inbox[7 + lax.rem(self.peers.tp + distance, self.pieces)].astype(F32)
        out_ref[...] = total
        for copy in self.along() + [self.across(stage) for stage in range(3)]:
            copy.wait_send()


def backward_kernel(
    cot_ref, hot_ref, feats_ref, m_ref, mid_ref, a_win_ref, x0_ref, x2_ref,
    mlp_near_ref, mlp_far_ref, slope_ref, act_ref,
    q_ref, kv_ref, q_hat_ref, k_hat_ref, q_scale_ref, k_scale_ref, p_ref, attn_near_ref, attn_far_ref, heads_ref, o_ref,
    g_ref, up_grad_ref, head_sums_ref, mlp_sums_ref, norm_sums_ref, tally_ref, mlp_out, attn_out,
    gz_ref, gh_ref, g1_ref, gr_ref, acc_ref, window_ref, gq_ref, gkv_ref, turned_ref, a_t_ref,
    landed_ref, halo_send, halo_recv, free, fetched, chunks, inbox, tally_send, tally_recv, *buffers,
):
    layers, pieces, rows = up_grad_ref.shape[0], up_grad_ref.shape[1], g_ref.shape[0]
    half = g_ref.shape[1] // 2
    wide = slope_ref.shape[1]
    own = slice(REACH, REACH + rows)
    total_ref = window_ref.at[own]
    step = pl.program_id(0)
    peers = Neighbours()
    scatter_of = lambda layer, which: Scatter(
        peers, (mlp_out, attn_out)[which].at[layer], *buffers[8 * which : 8 * which + 6],
        *[item.at[layer] for item in buffers[8 * which + 6 : 8 * which + 8]],
    )
    back = lambda layer: Return(a_t_ref, landed_ref.at[layer], rows, halo_send.at[layer], halo_recv.at[layer])

    def fetch(source, target):
        copy = pltpu.make_async_copy(source, target, fetched)
        copy.start()
        copy.wait()

    def halo_back(layer):
        back(layer).end(total_ref)

    def made_free(item):
        layer, which = item
        scatter_of(layer + 1, which).done()
        for target in peers.all():
            pl.semaphore_signal(free.at[layer, which], inc=1, device_id=target, device_id_type=MESH)
        pl.semaphore_wait(free.at[layer, which], len(peers.all()))

    plan = Plan()
    plan.spend(2.5)
    halo_size = 2 * half * 2 * 2 * rows
    order = [(index + 1) % pieces for index in range(pieces)]
    for layer in reversed(range(layers)):
        for which in range(2):
            for index, piece in enumerate(order):
                at = (2 * (layers - 1 - layer) + which) * pieces + index
                if index == 0 and layer + 1 < layers:
                    if which == 0:
                        plan.wait(("halo", layer + 1), (halo_back, layer + 1), at, 0)
                    plan.finish(2 * (layers - 2 - layer) + which, at, 0)
                    plan.table.setdefault((at, 0), []).append((made_free, (layer, which)))
                plan.slot(at, 0)
                for slot, time in enumerate(((1.5,), (2.2, 1.3, 1.3))[which]):
                    plan.spend(time)
                    plan.slot(at, slot + 1)
                plan.spend((2.6, 3.0)[which])
                scatter_of(layer, which).made(plan, 2 * (layers - 1 - layer) + which, piece)
        plan.carry([("z", halo_size)], ("halo", layer))
    ending = 2 * layers * pieces
    plan.wait(("halo", 0), (halo_back, 0), ending, 0)
    plan.spend(8.0)
    tally = Tally(peers, chunks, inbox, tally_send, tally_recv, pieces)
    size = chunks.shape[1] * PAIR * 2
    for stage, (link, count) in enumerate((("core", 4), ("y", 2), ("x", 1), ("z", pieces))):
        plan.carry([(link, count * size)], ("tally", stage))
        work = (tally.fold, stage) if stage < 3 else (tally.total, tally_ref)
        plan.wait(("tally", stage), work, ending, 1)
    plan.finish(None, ending, 1)
    table = plan.table

    def run(at, slot):
        if (at, slot) in table:

            @pl.when(step == at)
            def _():
                for work, item in table[at, slot]:
                    work(item)

    phase = step // pieces
    layer = jnp.maximum(layers - 1 - phase // 2, 0)
    index = lax.rem(step, pieces)
    piece = lax.rem(index + 1, pieces)
    in_mlp, in_attend = lax.rem(phase, 2) == 0, lax.rem(phase, 2) == 1
    is_ending = step == ending

    @pl.when(step == 0)
    def _():
        peers.greet()
        fetch(cot_ref, g_ref)

    run(ending, 0)
    for at in range(2 * pieces, ending, 2 * pieces):
        run(at, 0)

    def through_norm(layer, x):
        fetch(x, acc_ref)
        total = total_ref[...]
        hat, scale = row_norm(acc_ref[...])
        g_ref[...] = g1_ref[...] + row_norm_back(total * line(feats_ref.at[layer], LN_GAIN[0]), hat, scale)
        norm_sums_ref[layer] = jnp.zeros(norm_sums_ref.shape[1:], F32)
        norm_sums_ref[layer, 0:1, :] = jnp.sum(total * hat, axis=0, keepdims=True)
        norm_sums_ref[layer, 1:2, :] = jnp.sum(total, axis=0, keepdims=True)

    for above in range(1, layers):

        @pl.when(step == 2 * (layers - above) * pieces)
        def _():
            through_norm(above, x2_ref.at[above - 1])

    @pl.when(is_ending)
    def _():
        through_norm(0, x0_ref)
        tables = split_dot(hot_ref[...].T, g_ref[...])
        tally.build(tables, total_ref, acc_ref, norm_sums_ref, mlp_sums_ref, head_sums_ref, up_grad_ref)

    @pl.when(jnp.logical_and(in_mlp, step < ending))
    def _():
        def hook(slot):
            for at in range(ending):
                if at // pieces % 2 == 0 and not (slot == 0 and at % (2 * pieces) == 0 and at):
                    run(at, slot)

        hook(0)
        up, down = pl.ds(0, wide), pl.ds(wide, wide)
        mlp_back_work(
            g_ref, mlp_near_ref.at[:, down], mlp_far_ref.at[:, down], slope_ref, mlp_near_ref.at[:, up], mlp_far_ref.at[:, up],
            mid_ref, feats_ref.at[layer], gz_ref, gh_ref, up_grad_ref.at[layer, piece], g1_ref, gr_ref,
            mlp_sums_ref.at[layer], acc_ref, index == 0, index == pieces - 1, hook,
        )

        @pl.when(index == 0)
        def _():
            turned_ref[0] = m_ref[...].T
            turned_ref[1] = gz_ref[...].T

        away, keep = buffers[0], buffers[1]
        scatter = scatter_of(layer, 0)
        scatter.room(index, piece)
        for part, ref in ((slice(0, half), keep.at[piece]), (slice(half, 2 * half), away.at[scatter.slot(piece)])):
            ref[:, :wide] = nn(turned_ref[0, part, :], gh_ref[...]).astype(BF16)
            ref[:, wide:] = nn(turned_ref[1, part, :], act_ref[...]).astype(BF16)
        scatter.start(piece, "core")

    @pl.when(in_attend)
    def _():
        def hook(slot):
            for at in range(ending):
                if at // pieces % 2 == 1:
                    run(at, slot)

        hook(0)

        @pl.when(index == 0)
        def _():
            window_ref[...] = jnp.zeros_like(window_ref)
            a_t_ref[...] = a_win_ref[...].T
            turned_ref[0] = gr_ref[...].T

        attend_back_work(
            gr_ref, q_ref, kv_ref, q_hat_ref, k_hat_ref, q_scale_ref, k_scale_ref, p_ref, attn_near_ref, attn_far_ref,
            heads_ref, gq_ref, gkv_ref, head_sums_ref.at[layer, piece], window_ref, hook,
        )
        away, keep = buffers[8], buffers[9]
        scatter = scatter_of(layer, 1)
        scatter.room(index, piece)
        for part, ref in ((slice(0, half), keep.at[piece]), (slice(half, 2 * half), away.at[scatter.slot(piece)])):
            from_q = nn(a_t_ref[part, own], gq_ref[...])
            from_o = nn(turned_ref[0, part, :], o_ref[...])
            ref[:, :PAIR] = from_q[:, :PAIR].astype(BF16)
            ref[:, PAIR : 4 * PAIR] = nn(a_t_ref[part, :], gkv_ref[...]).astype(BF16)
            ref[:, 4 * PAIR : 5 * PAIR] = (from_q[:, PAIR:] + from_o[:, :PAIR]).astype(BF16)
            ref[:, 5 * PAIR :] = from_o[:, PAIR:].astype(BF16)
        scatter.start(piece, "core")

        @pl.when(index == pieces - 1)
        def _():
            a_t_ref[:REACH, : 2 * half] = window_ref[:REACH, :].astype(BF16)
            a_t_ref[REACH : 2 * REACH, : 2 * half] = window_ref[REACH + rows :, :].astype(BF16)
            back(layer).begin()

    run(ending, 1)

    @pl.when(is_ending)
    def _():
        for which in range(2):
            scatter_of(0, which).done()


def scatter_buffers(layers, pieces, chunk, wide):
    buffer = lambda rows: pltpu.VMEM((pieces, rows * chunk, wide), BF16)
    semaphores = pltpu.SemaphoreType.DMA((layers, pieces, Scatter.KINDS))
    away = pltpu.VMEM((2, 4 * chunk, wide), BF16)
    given = pltpu.VMEM((pieces - 1, chunk, wide), BF16)
    return [away, buffer(4), buffer(4), buffer(2), buffer(1), given, semaphores, semaphores]


def backward(cotangent, hot, lines, feats, heads, start, saved):
    *stored, o, act, slope, mid, m, x2, a_win, attn_near, attn_far, mlp_near, mlp_far = saved
    layers, window, width = a_win.shape
    rows, half, pieces = m.shape[1], width // 2, attn_near.shape[1]
    hidden = act.shape[2]
    wide, chunk = hidden // pieces, half // 4

    def mlp_at(step):
        phase = jnp.minimum(step // pieces, 2 * layers - 1)
        index = jnp.where(lax.rem(phase, 2) == 0, lax.rem(step, pieces), pieces - 1)
        return layers - 1 - phase // 2, lax.rem(index + 1, pieces)

    def attend_at(step):
        phase = jnp.minimum(step // pieces, 2 * layers - 1)
        index = jnp.where(lax.rem(phase, 2) == 1, lax.rem(step, pieces), 0)
        index = jnp.where(step == 2 * layers * pieces, pieces - 1, index)
        return layers - 1 - phase // 2, lax.rem(index + 1, pieces)

    once = lambda shape: pl.BlockSpec(shape, lambda step: (0,) * len(shape), pipeline_mode=pl.Buffered(1))
    weight = lambda at, wide: pl.BlockSpec((None, None, half, wide), lambda step: (*at(step), 0, 0))
    cols = lambda at, height, wide: pl.BlockSpec((None, height, wide), lambda step: (at(step)[0], 0, at(step)[1]))
    by_heads = pl.BlockSpec((3, window, rows), lambda step: (attend_at(step)[0] * pieces + attend_at(step)[1], 0, 0))
    layer_heads = pl.BlockSpec((None, None, HEADS, 3 * PAIR), lambda step: (attend_at(step)[1], attend_at(step)[0], 0, 0))
    layer_sheet = lambda at, height: pl.BlockSpec(
        (None, height, width), lambda step: (at(step)[0], 0, 0), pipeline_mode=pl.Buffered(1)
    )
    outs = [
        (rows, width), (layers, pieces, 1, wide), (layers, pieces, 8, 3 * PAIR), (layers, 8, width), (layers, 8, width),
        (lines, PAIR), (layers, chunk, 2 * wide), (layers, chunk, 6 * PAIR),
    ]
    vmem = lambda shape, kind=BF16: pltpu.VMEM(shape, kind)
    inputs = (cotangent, hot, feats, m, mid, a_win, start, x2, mlp_near, mlp_far, slope, act, *stored, attn_near, attn_far, heads, o)
    return pl.pallas_call(
        backward_kernel,
        grid=(2 * layers * pieces + 1,),
        in_specs=[
            ANY, once(hot.shape), once(feats.shape), layer_sheet(mlp_at, rows), layer_sheet(mlp_at, rows), layer_sheet(attend_at, window), ANY, ANY,
            weight(mlp_at, 2 * wide), weight(mlp_at, 2 * wide), cols(mlp_at, rows, wide),
            cols(mlp_at, rows, wide), *[cols(attend_at, *shape) for shape in attend_shapes(rows, window)], by_heads,
            weight(attend_at, 6 * PAIR), weight(attend_at, 6 * PAIR), layer_heads, cols(attend_at, rows, 2 * PAIR),
        ],
        out_specs=[once(shape) for shape in outs],
        out_shape=[shaped(shape, F32) for shape in outs],
        scratch_shapes=[
            vmem((rows, width)), vmem((rows, wide)), vmem((rows, width), F32), vmem((rows, width)),
            vmem((rows, width), F32), vmem((window, width), F32), vmem((rows, 2 * PAIR)), vmem((window, 3 * PAIR)),
            vmem((2, width, rows)), vmem((width, window)),
            vmem((layers, 2 * REACH, width)), pltpu.SemaphoreType.DMA((layers, 4)), pltpu.SemaphoreType.DMA((layers, 4)),
            pltpu.SemaphoreType.REGULAR((layers, 2)), pltpu.SemaphoreType.DMA, vmem((8, lines, PAIR)),
            vmem((7 + pieces, lines, PAIR)), pltpu.SemaphoreType.DMA((pieces + 2,)), pltpu.SemaphoreType.DMA((pieces + 2,)), *scatter_buffers(layers, pieces, chunk, 2 * wide),
            *scatter_buffers(layers, pieces, chunk, 6 * PAIR),
        ],
        compiler_params=params(40, VMEM),
        name="backward",
    )(*inputs)


def flip(array, bit, axis="fsdp"):
    size = lax.axis_size(axis)
    return lax.ppermute(array, axis, [(i, i ^ (1 << bit)) for i in range(size)])


def ring(array):
    size = lax.axis_size("tp")
    return lax.ppermute(array, "tp", [(i, (i + 1) % size) for i in range(size)])


def hop(array, distance):
    size = lax.axis_size("tp")
    return lax.ppermute(array, "tp", [(i, i + distance) for i in range(size) if 0 <= i + distance < size])


def bits_of(size):
    return size.bit_length() - 1


def row_bits(first_top):
    count = bits_of(lax.axis_size("fsdp"))
    tops = [count - 1, count - 2] if first_top else [count - 2, count - 1]
    return list(range(1, count - 2)), tops


def gather_by_permutes(block, first_top):
    pieces = [block]
    for _ in range(lax.axis_size("tp") - 1):
        pieces.append(ring(pieces[-1]))
    block = jnp.concatenate(pieces, axis=1)
    low, tops = row_bits(first_top)
    have = []
    for bit in low + tops:
        axis = sum(other > bit for other in have)
        block = jnp.stack([block, flip(block, bit)], axis=axis)
        have.append(bit)
    block = block.reshape((-1, len(pieces), pieces[0].shape[1])).transpose(1, 0, 2)[None]
    return block, flip(block, 0)


def add(left, right, kind=BF16):
    return (left.astype(F32) + right.astype(F32)).astype(kind)


def reduce_by_permutes(keep, send, first_top):
    low, tops = row_bits(first_top)
    block = add(keep, flip(send, 0))
    order = tops + low[::-1]
    have = sorted(order, reverse=True)
    block = block.reshape((2,) * len(have) + (-1, block.shape[-1]))
    for bit in order:
        axis = have.index(bit)
        mine = lax.index_in_dim(block, 0, axis, keepdims=False)
        other = lax.index_in_dim(block, 1, axis, keepdims=False)
        block = add(mine, flip(other, bit))
        have.remove(bit)
    pieces = jnp.split(block, lax.axis_size("tp"), axis=1)
    total = pieces[1]
    for piece in pieces[2:]:
        total = add(ring(total), piece)
    return add(ring(total), pieces[0], F32)


def attn_shard(w_qkv, w_out):
    q, k, v = (w_qkv[:, which] for which in range(3))
    o = w_out.T
    return side(q[:, :PAIR], k[:, :PAIR], v[:, :PAIR], k[:, PAIR:], v[:, PAIR:], q[:, PAIR:], o[:, PAIR:], o[:, :PAIR])


def attn_unshard(block):
    tile = lambda start, wide=PAIR: block[:, start : start + wide]
    q = side(tile(0), tile(4 * PAIR, HD))
    k = side(tile(PAIR), tile(3 * PAIR, HD))
    v = side(tile(2 * PAIR), tile(3 * PAIR + HD, HD))
    o = side(tile(5 * PAIR), tile(4 * PAIR + HD, HD))
    return jnp.stack([q, k, v], axis=1), o.T


def body(
    tokens, segment_ids, patch_pos, row_table, col_table, ln_gain, ln_bias, qkv_bias, qk_gain, query_bias, out_bias,
    fc1_bias, fc2_bias, w_qkv, w_out, w_fc1, w_fc2, cotangent,
):
    layers = w_qkv.shape[0]
    rows, width = tokens.shape
    half = width // 2
    fsdp, tp = lax.axis_size("fsdp"), lax.axis_size("tp")
    f_index, t_index = lax.axis_index("fsdp"), lax.axis_index("tp")
    hidden = fc1_bias.shape[1] * fsdp * tp
    grid = row_table.shape[0]
    fine = width // (fsdp * tp)
    parts = hidden // width
    in_kernel = fsdp == 8

    place = jnp.arange(width, dtype=jnp.int32)
    chunk = width // fsdp
    slot = place // chunk
    away = (slot % (fsdp // 2)) * 2 + slot // (fsdp // 2)
    feature_at = (f_index ^ away) * chunk + place % chunk
    head_cols = width // tp
    spot = jnp.arange(tp * 3 * PAIR, dtype=jnp.int32)
    tile, part = spot % (3 * PAIR) // PAIR, spot % PAIR // HD
    head = jnp.where(tile == 0, part, jnp.where(tile == part + 1, 2, -fsdp * tp))
    head_at = ((t_index - spot // (3 * PAIR)) % tp) * head_cols + head * HD + spot % HD
    to_feature = (place[:, None] == feature_at[None, :]).astype(BF16)
    to_head = (place[:, None] == head_at[None, :]).astype(BF16)
    device = jnp.arange(fsdp * tp, dtype=jnp.int32)
    wanted = ((t_index - device // fsdp) % tp) * fsdp + device % fsdp
    to_hidden = (wanted[:, None] == device[None, :]).astype(BF16)

    by_layer = lambda *items: jnp.concatenate([item.reshape(layers, -1, fine) for item in items], axis=1).reshape(-1, fine)
    shares = [
        row_table, col_table, by_layer(ln_gain, ln_bias, out_bias, fc2_bias), by_layer(qkv_bias, qk_gain, query_bias),
        fc1_bias.reshape(layers * parts, fine),
    ]
    count = sum(item.shape[0] for item in shares)
    attn_shards = jnp.stack([attn_shard(w_qkv[layer], w_out[layer]) for layer in range(layers)])
    mlp_shards = jnp.concatenate([w_fc1, w_fc2.transpose(0, 2, 1)], axis=2)
    grid_ids = jnp.arange(grid, dtype=jnp.int32)
    row_hot = patch_pos[0][:, None] == grid_ids[None, :]
    col_hot = patch_pos[1][:, None] == grid_ids[None, :]
    hot = side(row_hot, col_hot).astype(BF16)
    tokens = jnp.dot(tokens, to_feature, preferred_element_type=F32)
    segments = segment_ids[0]
    padded = jnp.pad(segments, (REACH, REACH), constant_values=-1)
    seg_k = lax.dynamic_slice_in_dim(padded, t_index * rows, rows + 2 * REACH).reshape(-1, 1)
    seg_q = lax.dynamic_slice_in_dim(segments, t_index * rows, rows).reshape(1, -1)
    spill = REACH - rows

    if in_kernel:
        share = jnp.concatenate([jnp.pad(item, ((0, -item.shape[0] % 16), (0, PAIR - fine))) for item in shares], axis=0)
        *kept, start, feats, heads, a_win, attn_near, attn_far, mlp_near, mlp_far = forward(
            tokens, hot, share, seg_k, seg_q, attn_shards, mlp_shards
        )
        residual = kept[-1][layers - 1]
        kept += [a_win, attn_near, attn_far, mlp_near, mlp_far]
    else:
        small = jnp.concatenate(shares, axis=0)
        flat = small.reshape(1, -1)
        for bit in range(bits_of(tp)):
            flat = jnp.concatenate([flat, flip(flat, bit, "tp")], axis=0)
        for bit in range(bits_of(fsdp)):
            flat = jnp.concatenate([flat, flip(flat, bit)], axis=0)
        flat = flat[jnp.arange(fsdp * tp) ^ (f_index * tp + t_index)]
        gathered = flat.reshape(fsdp * tp, count, fine)
        lined = gathered.transpose(1, 0, 2).reshape(count, width)
        wide = 2 * grid + 6 * layers
        feats = jnp.dot(lined[:wide], to_feature, preferred_element_type=F32)
        heads = jnp.dot(lined[wide : wide + 6 * layers], to_head, preferred_element_type=F32)
        up_shift = jnp.einsum(
            "or,rlsi->losi",
            to_hidden,
            gathered[:, wide + 6 * layers :].reshape(fsdp * tp, layers, parts, fine),
            preferred_element_type=F32,
        ).reshape(layers, tp, 1, hidden // tp)
        tables = feats[: 2 * grid].astype(BF16)
        feats = feats[2 * grid :].reshape(layers, FEATS, width)

        heads = heads.reshape(layers, HEADS, tp, 3 * PAIR).transpose(2, 0, 1, 3)
        residual = tokens + jnp.dot(hot, tables, preferred_element_type=F32)
        hat, _ = row_norm(residual)
        a_own = (hat * feats[0, LN_GAIN[0]] + feats[0, LN_BIAS[0]]).astype(BF16)
        saved = []
        for layer in range(layers):
            a_win = jnp.concatenate(
                [hop(a_own[rows - spill :], 2), hop(a_own, 1), a_own, hop(a_own, -1), hop(a_own[:spill], -2)], axis=0
            )
            attn_near, attn_far = gather_by_permutes(attn_shards[layer], layer % 2 == 0)
            *stored, probs, o, mid, m = attend(
                a_win, attn_near, attn_far, heads, feats, residual, seg_k, seg_q, layer
            )
            mlp_near, mlp_far = gather_by_permutes(mlp_shards[layer], layer % 2 == 1)
            act, slope, x2 = mlp(m, mid, mlp_near, mlp_far, up_shift, feats, layer)
            stored = [item[None] for item in stored] + [probs]
            kept = [item[None] for item in (o, mid, m, act, slope)]
            saved.append((residual, a_win[None], stored, *kept, attn_near, attn_far, mlp_near, mlp_far))
            residual = x2
            if layer + 1 < layers:
                hat, _ = row_norm(residual)
                a_own = (
                    hat * feats[layer + 1, LN_GAIN[0]] + feats[layer + 1, LN_BIAS[0]]
                ).astype(BF16)

    restore = functools.partial(
        lax.dot_general, dimension_numbers=(((1,), (1,)), ((), ())), precision=HIGHEST, preferred_element_type=F32
    )
    exact = to_feature.astype(F32)
    activations = restore(residual, exact)
    cotangent_here = jnp.dot(cotangent, exact, precision=HIGHEST, preferred_element_type=F32)
    kept_sums = [None] * layers
    if in_kernel:
        grad, _, _, _, _, tally, mlp_blocks, attn_blocks = backward(
            cotangent_here, hot, share.shape[0], feats, heads, start, kept
        )
    else:
        grad, mlp_blocks, attn_blocks = cotangent_here, [None] * layers, [None] * layers
        for layer in reversed(range(layers)):
            x, a_win, stored, o, mid, m, act, slope, attn_near, attn_far, mlp_near, mlp_far = saved[layer]
            gz, gh, up_grad, g1, gr, mlp_small = mlp_back(grad, mlp_near, mlp_far, slope, mid, feats, layer, 0)
            mlp_blocks[layer] = reduce_by_permutes(*mlp_weight_grads(m, gh, gz, act), layer % 2 == 0)
            gq, gkv, mine, left, right, attn_small = attend_back(gr, stored, attn_near, attn_far, heads, layer, 0)
            attn_blocks[layer] = reduce_by_permutes(*attn_weight_grads(a_win, gq, gkv, gr, o), layer % 2 == 1)
            ends = jnp.concatenate([hop(right[rows:], 2), hop(left[:spill], -2)], axis=0).astype(F32)
            attn_grad = mine + hop(right[:rows], 1).astype(F32) + hop(left[spill:], -1).astype(F32) + ends
            hat, scale = row_norm(x)
            grad = g1 + row_norm_back(attn_grad * feats[layer, LN_GAIN[0]], hat, scale)
            kept_sums[layer] = (
                jnp.sum(attn_grad * hat, axis=0), jnp.sum(attn_grad, axis=0), mlp_small, attn_small,
                up_grad.reshape(parts, width),
            )
    middle = mlp_blocks[0].shape[1] // 2
    w_fc1_grad = [block[:, :middle] for block in mlp_blocks]
    w_fc2_grad = [block[:, middle:].T for block in mlp_blocks]
    w_qkv_grad, w_out_grad = zip(*[attn_unshard(block) for block in attn_blocks])

    token_grad = restore(grad, exact)
    if in_kernel:
        found = lax.dynamic_slice_in_dim(tally, t_index * fine, fine, axis=1)
        rows_g, cols_g, rest = found[:grid], found[grid : 2 * grid], found[2 * grid :]
        by_feature = rest[: layers * FEATS].reshape(layers, FEATS, fine)
        by_head = rest[16 : 16 + layers * HEADS].reshape(layers, HEADS, fine)
        up_g = rest[32 : 32 + layers * parts].reshape(layers, parts * fine)
    else:
        row_grad = jnp.einsum("tg,td->gd", row_hot.astype(F32), grad, precision=HIGHEST)
        col_grad = jnp.einsum("tg,td->gd", col_hot.astype(F32), grad, precision=HIGHEST)
        featured = [row_grad, col_grad]
        headed = []
        for a_gain, a_shift, sums, head_sums, _ in kept_sums:
            featured.append(jnp.stack([a_gain, sums[2], a_shift, sums[3], sums[1], sums[0]]))
            headed += [head_sums[3:6], head_sums[0:2], head_sums[2:3]]
        headed = jnp.concatenate(headed)
        spread = jnp.concatenate(
            [restore(jnp.concatenate(featured), to_feature.astype(F32)), restore(headed, to_head.astype(F32))]
        )
        spread = spread.reshape(-1, fsdp * tp, fine).transpose(1, 0, 2)
        up_all = jnp.stack([item[4] for item in kept_sums]).reshape(layers, fsdp * tp, parts * fine)
        up_all = jnp.einsum("or,lok->rlk", to_hidden.astype(F32), up_all, precision=HIGHEST)
        flat = jnp.concatenate([spread.reshape(fsdp * tp, -1), up_all.reshape(fsdp * tp, -1)], axis=1)
        flat = flat[jnp.arange(fsdp * tp) ^ (f_index * tp + t_index)]
        for bit in reversed(range(bits_of(fsdp))):
            middle = flat.shape[0] // 2
            flat = flat[:middle] + flip(flat[middle:], bit)
        for bit in reversed(range(bits_of(tp))):
            middle = flat.shape[0] // 2
            flat = flat[:middle] + flip(flat[middle:], bit, "tp")
        found = flat.reshape(-1, fine)
        rows_g, cols_g, rest = found[:grid], found[grid : 2 * grid], found[2 * grid :]
        by_feature = rest[: layers * FEATS].reshape(layers, FEATS, fine)
        by_head = rest[layers * FEATS : layers * (FEATS + HEADS)].reshape(layers, HEADS, fine)
        up_g = rest[layers * (FEATS + HEADS) :].reshape(layers, parts * fine)
    gain_g, shift_g, out_g, last_g = by_feature[:, :2], by_feature[:, 2:4], by_feature[:, OUT_BIAS], by_feature[:, LAST_BIAS]
    proj_g, head_gain_g, head_shift_g = by_head[:, :3], by_head[:, 3:5], by_head[:, HEAD_BIAS]
    return (
        activations, token_grad, rows_g, cols_g, gain_g, shift_g, proj_g, head_gain_g, head_shift_g, out_g, up_g, last_g,
        jnp.stack(w_qkv_grad), jnp.stack(w_out_grad), jnp.stack(w_fc1_grad), jnp.stack(w_fc2_grad),
    )


def solution(mesh):
    both = ("fsdp", "tp")
    in_specs = (
        P(both, None), P("fsdp", None), P(None, both), P(None, both), P(None, both), P(None, None, both),
        P(None, None, both), P(None, None, both), P(None, None, both), P(None, both), P(None, both), P(None, both),
        P(None, both), P(None, "fsdp", None, "tp"), P(None, "tp", "fsdp"), P(None, "fsdp", "tp"), P(None, "tp", "fsdp"),
        P(both, None),
    )
    out_specs = (
        P(both, None), P(both, None), P(None, both), P(None, both), P(None, None, both), P(None, None, both),
        P(None, None, both), P(None, None, both), P(None, both), P(None, both), P(None, both), P(None, both),
        P(None, "fsdp", None, "tp"), P(None, "tp", "fsdp"), P(None, "fsdp", "tp"), P(None, "tp", "fsdp"),
    )
    return jax.shard_map(body, mesh=mesh, in_specs=in_specs, out_specs=out_specs, check_vma=False)
```

profile of v0, /device:TPU:0, one launch (start us, length us, event | category | flops | bytes accessed | tf_op | source)
XLA Modules:
  0.0 376.2 jit_solution(11265940644710333079)
XLA Ops:
  0.7 1.1 slice_bitcast_fusion.9
  1.8 0.8 fusion.32
  2.7 0.1 copy.65
  2.8 0.1 concatenate.49
  3.0 0.1 copy.66
  3.1 0.0 copy-start.6
  3.1 0.0 copy-start.19
  3.2 0.0 copy-start.20
  3.2 0.1 concatenate.50
  3.4 0.7 pad_maximum_fusion.4.attn_shard_ref
  4.1 0.1 pad_dynamic-slice_fusion
  4.2 1.0 copy.57.seg_k_ref
  5.2 0.6 constant_dynamic-slice_fusion.1.seg_q_ref
  5.8 0.1 iota_compare_fusion.9
  5.9 0.7 add_convert_fusion.hot_ref
  6.7 1.5 fusion.5.token_ref
  8.2 0.9 pad_maximum_fusion.mlp_shard_ref
  9.1 0.1 copy.49
  9.2 0.6 pad_dynamic-update-slice_fusion.1
  9.8 0.1 copy.50
  9.9 0.6 pad_dynamic-update-slice_fusion
  10.6 0.6 constant_dynamic-update-slice_fusion.2
  11.3 0.6 constant_dynamic-update-slice_fusion.1
  11.9 0.1 reshape.120
  12.0 0.6 constant_dynamic-update-slice_fusion.share_ref
  12.6 165.2 %forward.1 = (bf16[2,256,1024]{2,1,0:T(8,128)(2,1)}, bf16[2,1024,1536]{2,1,0:T(8,128)(2,1)}, bf16[2,256,1024]{2,1,0:T(8,128)(2,1)}, bf16[2,1024,1024]{2,1,0:T(8,...) custom-call(f32[256,768]{1,0:T(8,128)} %fusion.5.token_ref, ...), custom_call_target="tpu_custom_call" | custom-call | tf_op jit(solution)/shard_map/forward/pallas_call | solution.py:804
  177.7 3.3 fusion.4.cot_ref
  181.0 180.3 %backward.1 = (f32[256,768]{1,0:T(8,128)}, f32[2,4,1,768]{3,2,1,0:T(1,128)}, f32[2,4,8,384]{3,2,1,0:T(8,128)}, f32[2,8,768]{2,1,0:T(8,128)}, f32[2,8,768]{2,1,0:...) custom-call(f32[256,768]{1,0:T(8,128)} %fusion.4.cot_ref, ...), custom_call_target="tpu_custom_call" | custom-call | tf_op jit(solution)/shard_map/backward/pallas_call | solution.py:1561
  361.3 1.3 slice_bitcast_fusion.1
  362.7 0.9 pad_maximum_fusion.3
  363.6 0.9 pad_maximum_fusion.2
  364.5 0.1 fusion.29
  364.6 0.1 fusion.31
  364.8 0.8 copy.62
  365.8 0.9 pad_maximum_fusion.1
  366.6 2.2 fusion
  368.9 0.1 fusion.34
  368.9 0.7 copy.59
  369.6 0.7 copy.60
  370.3 0.1 fusion.33
  370.4 0.6 copy.61
  371.0 0.6 fusion.36
  371.5 0.6 fusion.35
  372.1 0.6 slice.273
  372.7 0.6 slice.274
  373.3 0.1 dynamic-slice.5
  373.3 0.6 reshape.124
  374.0 2.2 fusion.2
  (85 shorter events, 0.6 us)
Async XLA Ops:
  0.6 3.5 copy-start.5
  0.7 5.1 %copy-start.10 = (s32[2,256]{1,0:T(2,128)S(1)}, s32[2,256]{1,0:T(2,128)}, u32[]{:S(2)}) copy-start(s32[2,256]{1,0:T(2,128)} %param.20) | copy-start | bytes 6148
  0.7 6.0 %copy-start.18 = (bf16[256,768]{1,0:T(8,128)(2,1)S(1)}, bf16[256,768]{1,0:T(8,128)(2,1)}, u32[]{:S(2)}) copy-start(bf16[256,768]{1,0:T(8,128)(2,1)} %param.18) | copy-start | bytes 1179652
  2.7 5.5 %copy-start.2 = (bf16[2,768,96]{1,2,0:T(8,128)(2,1)S(1)}, bf16[2,768,96]{1,2,0:T(8,128)(2,1)}, u32[]{:S(2)}) copy-start(bf16[2,768,96]{1,2,0:T(8,128)(2,1)} %param.34) | copy-start | bytes 884740
  2.7 5.5 %copy-start.3 = (bf16[2,96,768]{2,1,0:T(8,128)(2,1)S(1)}, bf16[2,96,768]{2,1,0:T(8,128)(2,1)}, u32[]{:S(2)}) copy-start(bf16[2,96,768]{2,1,0:T(8,128)(2,1)} %param.33) | copy-start | bytes 884740
  3.1 6.0 %copy-start.6 = (bf16[64,24]{0,1:T(8,128)(2,1)S(1)}, bf16[64,24]{0,1:T(8,128)(2,1)}, u32[]{:S(2)}) copy-start(bf16[64,24]{0,1:T(8,128)(2,1)} %param.21) | copy-start | bytes 9220
  3.1 6.7 %copy-start.7 = (bf16[64,24]{0,1:T(8,128)(2,1)S(1)}, bf16[64,24]{0,1:T(8,128)(2,1)}, u32[]{:S(2)}) copy-start(bf16[64,24]{0,1:T(8,128)(2,1)} %param.22) | copy-start | bytes 9220
  3.1 7.4 %copy-start.19 = (bf16[2,24]{1,0:T(2,128)(2,1)S(1)}, bf16[2,24]{1,0:T(2,128)(2,1)}, u32[]{:S(2)}) copy-start(bf16[2,24]{1,0:T(2,128)(2,1)} %param.28) | copy-start | bytes 292
  3.2 7.4 %copy-start.20 = (bf16[2,24]{1,0:T(2,128)(2,1)S(1)}, bf16[2,24]{1,0:T(2,128)(2,1)}, u32[]{:S(2)}) copy-start(bf16[2,24]{1,0:T(2,128)(2,1)} %param.30) | copy-start | bytes 292
  3.2 7.4 %copy-start.13 = (bf16[2,2,24]{2,1,0:T(2,128)(2,1)S(1)}, bf16[2,2,24]{2,1,0:T(2,128)(2,1)}, u32[]{:S(2)}) copy-start(bf16[2,2,24]{2,1,0:T(2,128)(2,1)} %param.24) | copy-start | bytes 580
  3.2 7.4 %copy-start.14 = (bf16[2,2,24]{2,1,0:T(2,128)(2,1)S(1)}, bf16[2,2,24]{2,1,0:T(2,128)(2,1)}, u32[]{:S(2)}) copy-start(bf16[2,2,24]{2,1,0:T(2,128)(2,1)} %param.23) | copy-start | bytes 580
  3.3 7.9 %copy-start.12 = (bf16[2,2,24]{2,1,0:T(2,128)(2,1)S(1)}, bf16[2,2,24]{2,1,0:T(2,128)(2,1)}, u32[]{:S(2)}) copy-start(bf16[2,2,24]{2,1,0:T(2,128)(2,1)} %param.26) | copy-start | bytes 580
  3.3 7.9 %copy-start.11 = (bf16[2,3,24]{2,0,1:T(2,128)(2,1)S(1)}, bf16[2,3,24]{2,0,1:T(2,128)(2,1)}, u32[]{:S(2)}) copy-start(bf16[2,3,24]{2,0,1:T(2,128)(2,1)} %param.25) | copy-start | bytes 868
  3.3 7.9 %copy-start.15 = (bf16[2,24]{1,0:T(2,128)(2,1)S(1)}, bf16[2,24]{1,0:T(2,128)(2,1)}, u32[]{:S(2)}) copy-start(bf16[2,24]{1,0:T(2,128)(2,1)} %param.27) | copy-start | bytes 292
  3.3 8.5 %copy-start.16 = (bf16[2,96]{1,0:T(2,128)(2,1)S(1)}, bf16[2,96]{1,0:T(2,128)(2,1)}, u32[]{:S(2)}) copy-start(bf16[2,96]{1,0:T(2,128)(2,1)} %param.29) | copy-start | bytes 1156
  6.7 1.5 copy-start.8
  362.6 1.8 copy-start.1
  364.7 1.9 copy-start.9
  364.7 1.9 copy-start.17
  365.7 3.2 copy-start.4
  365.7 8.3 %copy-start = (f32[2,256,768]{2,1,0:T(8,128)S(1)}, f32[2,256,768]{2,1,0:T(8,128)}, u32[]{:S(2)}) copy-start(f32[2,256,768]{2,1,0:T(8,128)} %get-tuple-element.41.x2_ref) | copy-start | bytes 4718596
where the time goes:
time: 377 us; the launch traced here: 376 us
  Pallas kernels  345 us (92%)
  local copies, waits for them, and re-layouts  15.1 us (4%)
  matrix products  9.21 us (2%)
  other arithmetic  5.23 us (1%)
    pallas_call x1, Pallas kernels, backward(): pl.pallas_call(backward_kernel, grid=(2 * layers * pieces + 1,), in_specs...  180 us
    pallas_call x1, Pallas kernels, forward(): pl.pallas_call(forward_kernel, grid=(1 + 2 * layers * pieces,), in_specs=...  165 us

commit v1 on v0

--- a/solution.py
+++ b/solution.py
@@ -131,8 +131,8 @@
 class Plan:
     LINKS = {"x": (45.5e3, 1.5), "y": (45.5e3, 1.5), "z": (45.5e3, 2.2), "core": (600e3, 1.0)}
 
-    def __init__(self):
-        self.depth, self.clock = {"x": 5.0, "y": 5.0, "z": 5.0, "core": 20.0}, 0.0
+    def __init__(self, depth):
+        self.depth, self.clock = {"x": 3.0, "y": 3.0, "z": depth, "core": 20.0}, 0.0
         self.free, self.here, self.jobs, self.table = dict.fromkeys(self.LINKS, 0.0), {}, [], {}
 
     def add(self, rank, work, needs, copies, gives, group):
@@ -288,44 +288,63 @@
         self.place, self.size = lax.axis_index("tp"), lax.axis_size("tp")
         spill = REACH - rows
         self.moves = [
-            (1, pl.ds(REACH, rows), pl.ds(spill, rows)),
-            (-1, pl.ds(REACH, rows), pl.ds(REACH + rows, rows)),
-            (2, pl.ds(2 * rows, spill), pl.ds(0, spill)),
-            (-2, pl.ds(REACH, spill), pl.ds(REACH + 2 * rows, spill)),
+            (1, 1, pl.ds(REACH, rows), pl.ds(spill, rows)),
+            (-1, 1, pl.ds(REACH, rows), pl.ds(REACH + rows, rows)),
+            (1, 2, pl.ds(REACH - spill, spill), pl.ds(0, spill)),
+            (-1, 2, pl.ds(REACH + rows, spill), pl.ds(REACH + 2 * rows, spill)),
         ]
 
     def inside(self, distance):
         other = self.place + distance
         return jnp.logical_and(other >= 0, other < self.size)
 
+    def sends(self, index):
+        direction, far, *_ = self.moves[index]
+        return jnp.logical_and(self.inside(direction), self.inside(direction * (1 - far)))
+
+    def takes(self, index):
+        direction, far, *_ = self.moves[index]
+        return self.inside(-direction * far)
+
     def copy(self, index):
-        distance, source, target = self.moves[index]
+        direction, _, source, target = self.moves[index]
         return pltpu.make_async_remote_copy(
             src_ref=self.ref.at[source, :], dst_ref=self.ref.at[target, :], send_sem=self.send.at[index],
-            recv_sem=self.recv.at[index], device_id={"tp": self.place + distance}, device_id_type=MESH,
+            recv_sem=self.recv.at[index], device_id={"tp": self.place + direction}, device_id_type=MESH,
         )
 
+    def start(self, index):
+        @pl.when(self.sends(index))
+        def _():
+            self.copy(index).start()
+
+    def arrived(self, index):
+        @pl.when(self.takes(index))
+        def _():
+            self.copy(index).wait_recv()
+
     def begin(self):
-        for index, (distance, _, target) in enumerate(self.moves):
-
-            @pl.when(self.inside(distance))
-            def _():
-                self.copy(index).start()
-
-            @pl.when(jnp.logical_not(self.inside(-distance)))
+        for index in range(2):
+            self.start(index)
+        for index, (*_, target) in enumerate(self.moves):
+
+            @pl.when(jnp.logical_not(self.takes(index)))
             def _():
                 self.ref[target, :] = jnp.zeros((target.size, self.ref.shape[1]), BF16)
 
-    def end(self, _=None):
-        for index, (distance, _, _) in enumerate(self.moves):
-
-            @pl.when(self.inside(distance))
+    def relay(self):
+        for index in range(2):
+            self.arrived(index)
+            self.start(index + 2)
+
+    def end(self):
+        for index in range(4):
+            if index > 1:
+                self.arrived(index)
+
+            @pl.when(self.sends(index))
             def _():
                 self.copy(index).wait_send()
-
-            @pl.when(self.inside(-distance))
-            def _():
-                self.copy(index).wait_recv()
 
 
 def params(collective, memory=None):
@@ -615,6 +634,9 @@
     halo = lambda layer: Halo(a_win_ref.at[layer], rows, halo_send.at[layer], halo_recv.at[layer])
     keep_window = lambda layer: pltpu.make_async_copy(a_win_ref.at[layer], a_win_out.at[layer], kept.at[layer])
 
+    def relay(layer):
+        halo(layer).relay()
+
     def window(layer):
         halo(layer).end()
         keep_window(layer).start()
@@ -657,10 +679,9 @@
                 at = index * layers + layer
                 up_shift_ref[layer, index // 2, :, index % 2 * half : (index % 2 + 1) * half] = found[at : at + 1]
 
-    plan = Plan()
+    plan = Plan(1.0)
     for index, gather in enumerate(gathers):
         gather.jobs(plan, index)
-    halo_size = width * 2 * 2 * rows
     share_size = share_ref.shape[0] * PAIR * 2
     plan.spend(2.5)
     plan.carry([("z", pieces * share_size)], ("share", 0))
@@ -672,11 +693,14 @@
     plan.carry([("core", 4 * share_size)], ("share", 3))
     plan.wait(("share", 3), (open_up, 0), 0, 0)
     for layer in range(layers):
-        plan.carry([("z", halo_size)], ("halo", layer))
+        plan.carry([("z", width * 2 * rows)], ("near", layer))
         first = 1 + 2 * layer * pieces
         if layer == 0:
             plan.spend(5.0)
-        plan.wait(("halo", layer), (window, layer), *((first, 0) if layer else (0, 0)))
+        at = (first, 0) if layer else (0, 0)
+        plan.wait(("near", layer), (relay, layer), *at)
+        plan.carry([("z", width * 2 * (REACH - rows))], ("halo", layer))
+        plan.wait(("halo", layer), (window, layer), *at)
         for index in range(pieces):
             piece = turn(index, pieces)
             plan.wait(("core", 2 * layer, piece), (gathers[2 * layer].need, piece), first + index, 0)
@@ -1189,44 +1213,71 @@
     def __init__(self, edges, landed, rows, send, recv):
         self.edges, self.landed, self.send, self.recv = edges, landed, send, recv
         self.place, self.size = lax.axis_index("tp"), lax.axis_size("tp")
-        spill = REACH - rows
+        self.rows, self.spill = rows, REACH - rows
+        spill = self.spill
         self.moves = [
-            (1, 1, pl.ds(0, rows), pl.ds(0, rows), 0),
-            (-1, 0, pl.ds(spill, rows), pl.ds(rows, rows), 0),
-            (2, 1, pl.ds(rows, spill), pl.ds(2 * rows, spill), 0),
-            (-2, 0, pl.ds(0, spill), pl.ds(2 * rows + spill, spill), rows - spill),
+            (1, 2, REACH + rows, spill, 2 * rows),
+            (-1, 2, 0, spill, 2 * rows + spill),
+            (1, 1, REACH, rows, 0),
+            (-1, 1, spill, rows, rows),
         ]
 
     def inside(self, distance):
         other = self.place + distance
         return jnp.logical_and(other >= 0, other < self.size)
 
+    def sends(self, index):
+        direction, far, *_ = self.moves[index]
+        return self.inside(direction * far)
+
+    def takes(self, index):
+        direction, far, *_ = self.moves[index]
+        return jnp.logical_and(self.inside(-direction), self.inside(direction * (far - 1)))
+
     def copy(self, index):
-        distance, which, source, target, _ = self.moves[index]
+        direction, _, start, count, target = self.moves[index]
         return pltpu.make_async_remote_copy(
-            src_ref=self.edges.at[pl.ds(which * REACH + source.start, source.size), pl.ds(0, self.landed.shape[1])],
-            dst_ref=self.landed.at[target, :], send_sem=self.send.at[index],
-            recv_sem=self.recv.at[index], device_id={"tp": self.place + distance}, device_id_type=MESH,
+            src_ref=self.edges.at[pl.ds(start, count), pl.ds(0, self.landed.shape[1])],
+            dst_ref=self.landed.at[pl.ds(target, count), :], send_sem=self.send.at[index], recv_sem=self.recv.at[index],
+            device_id={"tp": self.place + direction}, device_id_type=MESH,
         )
 
+    def start(self, index):
+        @pl.when(self.sends(index))
+        def _():
+            self.copy(index).start()
+
     def begin(self):
-        for index, (distance, *_) in enumerate(self.moves):
-
-            @pl.when(self.inside(distance))
+        for index in range(2):
+            self.start(index)
+
+    def relay(self):
+        wide = self.landed.shape[1]
+        for index, into in ((0, REACH), (1, REACH - self.spill)):
+            target = self.moves[index][4]
+
+            @pl.when(self.takes(index))
             def _():
-                self.copy(index).start()
+                self.copy(index).wait_recv()
+                rows = slice(into, into + self.spill)
+                self.edges[rows, :wide] = self.edges[rows, :wide] + self.landed[target : target + self.spill, :]
+
+            self.start(index + 2)
 
     def end(self, total_ref):
-        for index, (distance, _, _, target, start) in enumerate(self.moves):
-
-            @pl.when(self.inside(distance))
+        for index in range(4):
+
+            @pl.when(self.sends(index))
             def _():
                 self.copy(index).wait_send()
 
-            @pl.when(self.inside(-distance))
+        for index in (2, 3):
+            target = self.moves[index][4]
+
+            @pl.when(self.takes(index))
             def _():
                 self.copy(index).wait_recv()
-                total_ref[pl.ds(start, target.size), :] += self.landed[target, :].astype(F32)
+                total_ref[...] += self.landed[target : target + self.rows, :].astype(F32)
 
 
 def split_dot(left, right):
@@ -1358,6 +1409,9 @@
         copy.start()
         copy.wait()
 
+    def pass_on(layer):
+        back(layer).relay()
+
     def halo_back(layer):
         back(layer).end(total_ref)
 
@@ -1368,9 +1422,14 @@
             pl.semaphore_signal(free.at[layer, which], inc=1, device_id=target, device_id_type=MESH)
         pl.semaphore_wait(free.at[layer, which], len(peers.all()))
 
-    plan = Plan()
+    plan = Plan(3.0)
     plan.spend(2.5)
-    halo_size = 2 * half * 2 * 2 * rows
+
+    def whole_return(layer, *at):
+        plan.wait(("far", layer), (pass_on, layer), *at)
+        plan.carry([("z", 4 * half * rows)], ("halo", layer))
+        plan.wait(("halo", layer), (halo_back, layer), *at)
+
     order = [(index + 1) % pieces for index in range(pieces)]
     for layer in reversed(range(layers)):
         for which in range(2):
@@ -1378,7 +1437,7 @@
                 at = (2 * (layers - 1 - layer) + which) * pieces + index
                 if index == 0 and layer + 1 < layers:
                     if which == 0:
-                        plan.wait(("halo", layer + 1), (halo_back, layer + 1), at, 0)
+                        whole_return(layer + 1, at, 0)
                     plan.finish(2 * (layers - 2 - layer) + which, at, 0)
                     plan.table.setdefault((at, 0), []).append((made_free, (layer, which)))
                 plan.slot(at, 0)
@@ -1387,9 +1446,9 @@
                     plan.slot(at, slot + 1)
                 plan.spend((2.6, 3.0)[which])
                 scatter_of(layer, which).made(plan, 2 * (layers - 1 - layer) + which, piece)
-        plan.carry([("z", halo_size)], ("halo", layer))
+        plan.carry([("z", 4 * half * (REACH - rows))], ("far", layer))
     ending = 2 * layers * pieces
-    plan.wait(("halo", 0), (halo_back, 0), ending, 0)
+    whole_return(0, ending, 0)
     plan.spend(8.0)
     tally = Tally(peers, chunks, inbox, tally_send, tally_recv, pieces)
     size = chunks.shape[1] * PAIR * 2

time: 377 us -> 356 us (0.944)
  Pallas kernels: 345 us -> 324 us
    pallas_call x1, Pallas kernels: 180 us -> 163 us  [backward(): pl.pallas_call(backward_kernel, grid=(2 * layers * pieces + 1,), in_specs...]
where the time goes in v1:
time: 356 us; the launch traced here: 355 us
  Pallas kernels  324 us (91%)
  local copies, waits for them, and re-layouts  15.1 us (4%)
  matrix products  9.22 us (3%)
  other arithmetic  5.23 us (1%)
    pallas_call x1, Pallas kernels, backward(): pl.pallas_call(backward_kernel, grid=(2 * layers * pieces + 1,), in_specs...  163 us
    pallas_call x1, Pallas kernels, forward(): pl.pallas_call(forward_kernel, grid=(1 + 2 * layers * pieces,), in_specs=...  161 us

profile of v1, /device:TPU:0, one launch (start us, length us, event | category | flops | bytes accessed | tf_op | source)
XLA Modules:
  0.0 355.2 jit_solution(17560061262637383672)
XLA Ops:
  0.7 1.1 slice_bitcast_fusion.9
  1.8 0.8 fusion.32
  2.7 0.1 copy.65
  2.8 0.1 concatenate.49
  3.0 0.1 copy.66
  3.1 0.0 copy-start.19
  3.2 0.0 copy-start.20
  3.2 0.1 concatenate.50
  3.3 0.0 copy-start.11
  3.4 0.7 pad_maximum_fusion.4.attn_shard_ref
  4.1 0.1 pad_dynamic-slice_fusion
  4.2 1.0 copy.57.seg_k_ref
  5.2 0.6 constant_dynamic-slice_fusion.1.seg_q_ref
  5.8 0.1 iota_compare_fusion.9
  5.9 0.7 add_convert_fusion.hot_ref
  6.7 1.5 fusion.5.token_ref
  8.2 0.9 pad_maximum_fusion.mlp_shard_ref
  9.1 0.1 copy.49
  9.2 0.6 pad_dynamic-update-slice_fusion.1
  9.8 0.1 copy.50
  9.9 0.6 pad_dynamic-update-slice_fusion
  10.6 0.6 constant_dynamic-update-slice_fusion.2
  11.3 0.6 constant_dynamic-update-slice_fusion.1
  11.9 0.1 reshape.120
  12.0 0.6 constant_dynamic-update-slice_fusion.share_ref
  12.6 161.5 %forward.1 = (bf16[2,256,1024]{2,1,0:T(8,128)(2,1)}, bf16[2,1024,1536]{2,1,0:T(8,128)(2,1)}, bf16[2,256,1024]{2,1,0:T(8,128)(2,1)}, bf16[2,1024,1024]{2,1,0:T(8,...) custom-call(f32[256,768]{1,0:T(8,128)} %fusion.5.token_ref, ...), custom_call_target="tpu_custom_call" | custom-call | tf_op jit(solution)/shard_map/forward/pallas_call | solution.py:828
  174.0 3.3 fusion.4.cot_ref
  177.3 163.0 %backward.1 = (f32[256,768]{1,0:T(8,128)}, f32[2,4,1,768]{3,2,1,0:T(1,128)}, f32[2,4,8,384]{3,2,1,0:T(8,128)}, f32[2,8,768]{2,1,0:T(8,128)}, f32[2,8,768]{2,1,0:...) custom-call(f32[256,768]{1,0:T(8,128)} %fusion.4.cot_ref, ...), custom_call_target="tpu_custom_call" | custom-call | tf_op jit(solution)/shard_map/backward/pallas_call | solution.py:1620
  340.3 1.3 slice_bitcast_fusion.1
  341.7 0.9 pad_maximum_fusion.3
  342.6 0.9 pad_maximum_fusion.2
  343.5 0.1 fusion.29
  343.6 0.1 fusion.31
  343.8 0.8 copy.62
  344.8 0.9 pad_maximum_fusion.1
  345.7 2.2 fusion
  347.9 0.1 fusion.34
  347.9 0.7 copy.59
  348.6 0.7 copy.60
  349.3 0.1 fusion.33
  349.4 0.6 copy.61
  350.0 0.6 fusion.36
  350.6 0.6 fusion.35
  351.1 0.6 slice.273
  351.7 0.6 slice.274
  352.3 0.1 dynamic-slice.5
  352.3 0.6 reshape.124
  353.0 2.2 fusion.2
  (85 shorter events, 0.6 us)
Async XLA Ops:
  0.6 3.5 copy-start.5
  0.7 5.1 %copy-start.10 = (s32[2,256]{1,0:T(2,128)S(1)}, s32[2,256]{1,0:T(2,128)}, u32[]{:S(2)}) copy-start(s32[2,256]{1,0:T(2,128)} %param.20) | copy-start | bytes 6148
  0.7 6.0 %copy-start.18 = (bf16[256,768]{1,0:T(8,128)(2,1)S(1)}, bf16[256,768]{1,0:T(8,128)(2,1)}, u32[]{:S(2)}) copy-start(bf16[256,768]{1,0:T(8,128)(2,1)} %param.18) | copy-start | bytes 1179652
  2.7 5.5 %copy-start.2 = (bf16[2,768,96]{1,2,0:T(8,128)(2,1)S(1)}, bf16[2,768,96]{1,2,0:T(8,128)(2,1)}, u32[]{:S(2)}) copy-start(bf16[2,768,96]{1,2,0:T(8,128)(2,1)} %param.34) | copy-start | bytes 884740
  2.7 5.5 %copy-start.3 = (bf16[2,96,768]{2,1,0:T(8,128)(2,1)S(1)}, bf16[2,96,768]{2,1,0:T(8,128)(2,1)}, u32[]{:S(2)}) copy-start(bf16[2,96,768]{2,1,0:T(8,128)(2,1)} %param.33) | copy-start | bytes 884740
  3.1 6.0 %copy-start.6 = (bf16[64,24]{0,1:T(8,128)(2,1)S(1)}, bf16[64,24]{0,1:T(8,128)(2,1)}, u32[]{:S(2)}) copy-start(bf16[64,24]{0,1:T(8,128)(2,1)} %param.21) | copy-start | bytes 9220
  3.1 6.7 %copy-start.7 = (bf16[64,24]{0,1:T(8,128)(2,1)S(1)}, bf16[64,24]{0,1:T(8,128)(2,1)}, u32[]{:S(2)}) copy-start(bf16[64,24]{0,1:T(8,128)(2,1)} %param.22) | copy-start | bytes 9220
  3.1 7.4 %copy-start.19 = (bf16[2,24]{1,0:T(2,128)(2,1)S(1)}, bf16[2,24]{1,0:T(2,128)(2,1)}, u32[]{:S(2)}) copy-start(bf16[2,24]{1,0:T(2,128)(2,1)} %param.28) | copy-start | bytes 292
  3.2 7.4 %copy-start.20 = (bf16[2,24]{1,0:T(2,128)(2,1)S(1)}, bf16[2,24]{1,0:T(2,128)(2,1)}, u32[]{:S(2)}) copy-start(bf16[2,24]{1,0:T(2,128)(2,1)} %param.30) | copy-start | bytes 292
  3.2 7.4 %copy-start.13 = (bf16[2,2,24]{2,1,0:T(2,128)(2,1)S(1)}, bf16[2,2,24]{2,1,0:T(2,128)(2,1)}, u32[]{:S(2)}) copy-start(bf16[2,2,24]{2,1,0:T(2,128)(2,1)} %param.24) | copy-start | bytes 580
  3.2 7.4 %copy-start.14 = (bf16[2,2,24]{2,1,0:T(2,128)(2,1)S(1)}, bf16[2,2,24]{2,1,0:T(2,128)(2,1)}, u32[]{:S(2)}) copy-start(bf16[2,2,24]{2,1,0:T(2,128)(2,1)} %param.23) | copy-start | bytes 580
  3.3 7.9 %copy-start.12 = (bf16[2,2,24]{2,1,0:T(2,128)(2,1)S(1)}, bf16[2,2,24]{2,1,0:T(2,128)(2,1)}, u32[]{:S(2)}) copy-start(bf16[2,2,24]{2,1,0:T(2,128)(2,1)} %param.26) | copy-start | bytes 580
  3.3 7.9 %copy-start.11 = (bf16[2,3,24]{2,0,1:T(2,128)(2,1)S(1)}, bf16[2,3,24]{2,0,1:T(2,128)(2,1)}, u32[]{:S(2)}) copy-start(bf16[2,3,24]{2,0,1:T(2,128)(2,1)} %param.25) | copy-start | bytes 868
  3.3 7.9 %copy-start.15 = (bf16[2,24]{1,0:T(2,128)(2,1)S(1)}, bf16[2,24]{1,0:T(2,128)(2,1)}, u32[]{:S(2)}) copy-start(bf16[2,24]{1,0:T(2,128)(2,1)} %param.27) | copy-start | bytes 292
  3.3 8.5 %copy-start.16 = (bf16[2,96]{1,0:T(2,128)(2,1)S(1)}, bf16[2,96]{1,0:T(2,128)(2,1)}, u32[]{:S(2)}) copy-start(bf16[2,96]{1,0:T(2,128)(2,1)} %param.29) | copy-start | bytes 1156
  6.7 1.5 copy-start.8
  341.6 1.8 copy-start.1
  343.7 1.9 copy-start.9
  343.7 1.9 copy-start.17
  344.7 3.2 copy-start.4
  344.7 8.3 %copy-start = (f32[2,256,768]{2,1,0:T(8,128)S(1)}, f32[2,256,768]{2,1,0:T(8,128)}, u32[]{:S(2)}) copy-start(f32[2,256,768]{2,1,0:T(8,128)} %get-tuple-element.41.x2_ref) | copy-start | bytes 4718596

commit v2 on v1

--- a/solution.py
+++ b/solution.py
@@ -129,7 +129,7 @@
 
 
 class Plan:
-    LINKS = {"x": (45.5e3, 1.5), "y": (45.5e3, 1.5), "z": (45.5e3, 2.2), "core": (600e3, 1.0)}
+    LINKS = {"x": (43.5e3, 2.0), "y": (43.5e3, 2.0), "z": (43.5e3, 3.5), "core": (600e3, 1.0)}
 
     def __init__(self, depth):
         self.depth, self.clock = {"x": 3.0, "y": 3.0, "z": depth, "core": 20.0}, 0.0
@@ -1825,11 +1825,11 @@
                 ).astype(BF16)
 
     restore = functools.partial(
-        lax.dot_general, dimension_numbers=(((1,), (1,)), ((), ())), precision=HIGHEST, preferred_element_type=F32
+        lax.dot_general, dimension_numbers=(((1,), (1,)), ((), ())), precision=lax.Precision.HIGH, preferred_element_type=F32
     )
     exact = to_feature.astype(F32)
     activations = restore(residual, exact)
-    cotangent_here = jnp.dot(cotangent, exact, precision=HIGHEST, preferred_element_type=F32)
+    cotangent_here = jnp.dot(cotangent, exact, precision=lax.Precision.HIGH, preferred_element_type=F32)
     kept_sums = [None] * layers
     if in_kernel:
         grad, _, _, _, _, tally, mlp_blocks, attn_blocks = backward(

time: 356 us -> 351 us (0.986)
  no operation moved by 1% of the time
where the time goes in v2:
time: 351 us; the launch traced here: 350 us
  Pallas kernels  321 us (91%)
  local copies, waits for them, and re-layouts  15.1 us (4%)
  matrix products  7.95 us (2%)
  other arithmetic  5.23 us (1%)
    pallas_call x1, Pallas kernels, backward(): pl.pallas_call(backward_kernel, grid=(2 * layers * pieces + 1,), in_specs...  162 us
    pallas_call x1, Pallas kernels, forward(): pl.pallas_call(forward_kernel, grid=(1 + 2 * layers * pieces,), in_specs=...  159 us

profile of v2, /device:TPU:0, one launch (start us, length us, event | category | flops | bytes accessed | tf_op | source)
XLA Modules:
  0.0 350.3 jit_solution(11526094757989047894)
XLA Ops:
  0.7 1.1 slice_bitcast_fusion.9
  1.8 0.8 fusion.32
  2.7 0.1 copy.65
  2.8 0.1 concatenate.49
  3.0 0.1 copy.66
  3.1 0.0 copy-start.6
  3.2 0.0 copy-start.20
  3.2 0.0 copy-start.13
  3.2 0.1 concatenate.50
  3.4 0.7 pad_maximum_fusion.4.attn_shard_ref
  4.1 0.1 pad_dynamic-slice_fusion
  4.2 1.0 copy.57.seg_k_ref
  5.2 0.6 constant_dynamic-slice_fusion.1.seg_q_ref
  5.8 0.1 iota_compare_fusion.9
  5.9 0.7 add_convert_fusion.hot_ref
  6.7 1.5 fusion.5.token_ref
  8.2 0.9 pad_maximum_fusion.mlp_shard_ref
  9.1 0.1 copy.49
  9.2 0.6 pad_dynamic-update-slice_fusion.1
  9.8 0.1 copy.50
  9.9 0.6 pad_dynamic-update-slice_fusion
  10.6 0.6 constant_dynamic-update-slice_fusion.2
  11.3 0.6 constant_dynamic-update-slice_fusion.1
  11.9 0.1 reshape.120
  12.0 0.6 constant_dynamic-update-slice_fusion.share_ref
  12.6 158.9 %forward.1 = (bf16[2,256,1024]{2,1,0:T(8,128)(2,1)}, bf16[2,1024,1536]{2,1,0:T(8,128)(2,1)}, bf16[2,256,1024]{2,1,0:T(8,128)(2,1)}, bf16[2,1024,1024]{2,1,0:T(8,...) custom-call(f32[256,768]{1,0:T(8,128)} %fusion.5.token_ref, ...), custom_call_target="tpu_custom_call" | custom-call | tf_op jit(solution)/shard_map/forward/pallas_call | solution.py:828
  171.4 2.8 fusion.4.cot_ref
  174.3 161.9 %backward.1 = (f32[256,768]{1,0:T(8,128)}, f32[2,4,1,768]{3,2,1,0:T(1,128)}, f32[2,4,8,384]{3,2,1,0:T(8,128)}, f32[2,8,768]{2,1,0:T(8,128)}, f32[2,8,768]{2,1,0:...) custom-call(f32[256,768]{1,0:T(8,128)} %fusion.4.cot_ref, ...), custom_call_target="tpu_custom_call" | custom-call | tf_op jit(solution)/shard_map/backward/pallas_call | solution.py:1620
  336.2 1.3 slice_bitcast_fusion.1
  337.6 0.9 pad_maximum_fusion.3
  338.5 0.9 pad_maximum_fusion.2
  339.4 0.1 fusion.29
  339.5 0.1 fusion.31
  339.7 0.8 copy.62
  340.7 0.9 pad_maximum_fusion.1
  341.5 1.8 fusion
  343.3 0.1 fusion.34
  343.4 0.7 copy.59
  344.1 0.7 copy.60
  344.8 0.1 fusion.33
  344.9 0.6 copy.61
  345.4 0.6 fusion.36
  346.0 0.6 fusion.35
  346.6 0.6 slice.273
  347.2 0.6 slice.274
  347.7 0.1 dynamic-slice.5
  347.8 0.6 reshape.124
  348.5 1.8 fusion.2
  (85 shorter events, 0.6 us)
Async XLA Ops:
  0.6 3.5 copy-start.5
  0.7 5.1 %copy-start.10 = (s32[2,256]{1,0:T(2,128)S(1)}, s32[2,256]{1,0:T(2,128)}, u32[]{:S(2)}) copy-start(s32[2,256]{1,0:T(2,128)} %param.20) | copy-start | bytes 6148
  0.7 6.0 %copy-start.18 = (bf16[256,768]{1,0:T(8,128)(2,1)S(1)}, bf16[256,768]{1,0:T(8,128)(2,1)}, u32[]{:S(2)}) copy-start(bf16[256,768]{1,0:T(8,128)(2,1)} %param.18) | copy-start | bytes 1179652
  2.7 5.5 %copy-start.2 = (bf16[2,768,96]{1,2,0:T(8,128)(2,1)S(1)}, bf16[2,768,96]{1,2,0:T(8,128)(2,1)}, u32[]{:S(2)}) copy-start(bf16[2,768,96]{1,2,0:T(8,128)(2,1)} %param.34) | copy-start | bytes 884740
  2.7 5.5 %copy-start.3 = (bf16[2,96,768]{2,1,0:T(8,128)(2,1)S(1)}, bf16[2,96,768]{2,1,0:T(8,128)(2,1)}, u32[]{:S(2)}) copy-start(bf16[2,96,768]{2,1,0:T(8,128)(2,1)} %param.33) | copy-start | bytes 884740
  3.1 6.0 %copy-start.6 = (bf16[64,24]{0,1:T(8,128)(2,1)S(1)}, bf16[64,24]{0,1:T(8,128)(2,1)}, u32[]{:S(2)}) copy-start(bf16[64,24]{0,1:T(8,128)(2,1)} %param.21) | copy-start | bytes 9220
  3.1 6.7 %copy-start.7 = (bf16[64,24]{0,1:T(8,128)(2,1)S(1)}, bf16[64,24]{0,1:T(8,128)(2,1)}, u32[]{:S(2)}) copy-start(bf16[64,24]{0,1:T(8,128)(2,1)} %param.22) | copy-start | bytes 9220
  3.1 7.4 %copy-start.19 = (bf16[2,24]{1,0:T(2,128)(2,1)S(1)}, bf16[2,24]{1,0:T(2,128)(2,1)}, u32[]{:S(2)}) copy-start(bf16[2,24]{1,0:T(2,128)(2,1)} %param.28) | copy-start | bytes 292
  3.2 7.4 %copy-start.20 = (bf16[2,24]{1,0:T(2,128)(2,1)S(1)}, bf16[2,24]{1,0:T(2,128)(2,1)}, u32[]{:S(2)}) copy-start(bf16[2,24]{1,0:T(2,128)(2,1)} %param.30) | copy-start | bytes 292
  3.2 7.4 %copy-start.13 = (bf16[2,2,24]{2,1,0:T(2,128)(2,1)S(1)}, bf16[2,2,24]{2,1,0:T(2,128)(2,1)}, u32[]{:S(2)}) copy-start(bf16[2,2,24]{2,1,0:T(2,128)(2,1)} %param.24) | copy-start | bytes 580
  3.2 7.4 %copy-start.14 = (bf16[2,2,24]{2,1,0:T(2,128)(2,1)S(1)}, bf16[2,2,24]{2,1,0:T(2,128)(2,1)}, u32[]{:S(2)}) copy-start(bf16[2,2,24]{2,1,0:T(2,128)(2,1)} %param.23) | copy-start | bytes 580
  3.3 7.9 %copy-start.12 = (bf16[2,2,24]{2,1,0:T(2,128)(2,1)S(1)}, bf16[2,2,24]{2,1,0:T(2,128)(2,1)}, u32[]{:S(2)}) copy-start(bf16[2,2,24]{2,1,0:T(2,128)(2,1)} %param.26) | copy-start | bytes 580
  3.3 7.9 %copy-start.11 = (bf16[2,3,24]{2,0,1:T(2,128)(2,1)S(1)}, bf16[2,3,24]{2,0,1:T(2,128)(2,1)}, u32[]{:S(2)}) copy-start(bf16[2,3,24]{2,0,1:T(2,128)(2,1)} %param.25) | copy-start | bytes 868
  3.3 7.9 %copy-start.15 = (bf16[2,24]{1,0:T(2,128)(2,1)S(1)}, bf16[2,24]{1,0:T(2,128)(2,1)}, u32[]{:S(2)}) copy-start(bf16[2,24]{1,0:T(2,128)(2,1)} %param.27) | copy-start | bytes 292
  3.3 8.5 %copy-start.16 = (bf16[2,96]{1,0:T(2,128)(2,1)S(1)}, bf16[2,96]{1,0:T(2,128)(2,1)}, u32[]{:S(2)}) copy-start(bf16[2,96]{1,0:T(2,128)(2,1)} %param.29) | copy-start | bytes 1156
  6.7 1.5 copy-start.8
  337.5 1.8 copy-start.1
  339.6 1.9 copy-start.9
  339.6 1.9 copy-start.17
  340.5 2.8 copy-start.4
  340.6 7.9 %copy-start = (f32[2,256,768]{2,1,0:T(8,128)S(1)}, f32[2,256,768]{2,1,0:T(8,128)}, u32[]{:S(2)}) copy-start(f32[2,256,768]{2,1,0:T(8,128)} %get-tuple-element.41.x2_ref) | copy-start | bytes 4718596
